TPU v7x, 128 devices: a whole 4x4x4 slice. The times are simulated.
128 devices in a mesh: seq: 32 (over y, x, core), tp: 4 (over z).
Axes of the slice: x: 4, y: 4, z: 4, core: 2. Of those that a mesh axis runs over, the one named last changes fastest.
Arguments:
- tokens: bfloat16 [8192, 1536], P('seq'), may hold values from -6 to 6
- doc_ids: int32 [8192], P('seq'), may hold values from 0 to 3, never falling along the last dimension, each value on 1 to 4096 neighbouring positions
- mix_gain: bfloat16 [1536], replicated, may hold values from 0.25 to 1.75
- zgate_proj: bfloat16 [1536, 3072], P(None, 'tp'), may hold values from -0.15625 to 0.15625
- xin_proj: bfloat16 [1536, 3072], P(None, 'tp'), may hold values from -0.15625 to 0.15625
- bc_proj: bfloat16 [1536, 256], replicated, may hold values from -0.15625 to 0.15625
- dt_proj: bfloat16 [1536, 48], P(None, 'tp'), may hold values from -0.15625 to 0.15625
- conv_x: bfloat16 [4, 3072], P(None, 'tp'), may hold values from -3 to 3
- conv_bc: bfloat16 [4, 256], replicated, may hold values from -3 to 3
- dt_bias: float32 [48], P('tp'), may hold values from -3 to -1
- decay_rate: float32 [48], P('tp'), may hold values from 0.0001 to 0.5
- skip_gain: float32 [48], P('tp'), may hold values from 1 to 16
- norm_gain: bfloat16 [3072], P('tp'), may hold values from 0.25 to 1.75
- out_proj: bfloat16 [3072, 1536], P('tp'), may hold values from -0.109375 to 0.109375
- moe_gain: bfloat16 [1536], replicated, may hold values from 0.25 to 1.75
- router: bfloat16 [1536, 64], replicated, may hold values from -0.15625 to 0.15625
- routes: int32 [8192, 6], P('seq'), may hold values from 0 to 63, all different within a row; in each aligned block of 256 rows (0 to 255, 256 to 511, ...) at most 48 rows name the same one
- expert_gate_up: bfloat16 [64, 2, 1536, 512], P('seq', None, None, 'tp'), may hold values from -0.15625 to 0.15625
- expert_down: bfloat16 [64, 512, 1536], P('seq', 'tp'), may hold values from -0.25 to 0.25
- shared_gate_up: bfloat16 [2, 1536, 1024], P(None, None, 'tp'), may hold values from -0.15625 to 0.15625
- shared_down: bfloat16 [1024, 1536], P('tp'), may hold values from -0.1875 to 0.1875
Outputs:
- mixed: bfloat16 [8192, 1536], P('seq', 'tp')
Inputs may be any that keep to these rules, and one draw needn't show every extreme that they name: `doc_ids`: Non-decreasing along the tokens; each prompt holds 1 to 4096 tokens, one exactly 4096. `routes`: in each aligned block of 256 rows (the rows of one index of seq) no expert is named by more than 48 rows, a bound that some block reaches.
All inputs are finite; a program needn't handle non-finite values.
Results may differ from a plain program's by a relative error of at most 0.013.
Values may be sent and summed in bfloat16 or wider, within the bound.
A program may use at most 128 MiB of HBM per device.

v0:
```python
import jax
import jax.numpy as jnp
from jax import lax
from jax.sharding import PartitionSpec as P

D = 1536
HEAD = 64
NSTATE = 128
DI = 3072


epsilon = 1e-05
highest = lax.Precision.HIGHEST


def from_behind(value, axis, steps):
    count = lax.axis_size(axis)
    initial, last = (max(0, -steps), min(count, count - steps))
    return lax.ppermute(value, axis, [(source, source + steps) for source in range(initial, last)])


def prefix(value, axis, join, neutral):
    count, mine = (lax.axis_size(axis), lax.axis_index(axis))
    pieces = jax.tree.map(lambda part: lax.all_gather(part, axis), value)
    running = jax.tree.map(
        lambda part, zero: jnp.full_like(part, 0) + jnp.asarray(zero, part.dtype), value, neutral
    )

    def turn(position, running):
        longer = join(running, jax.tree.map(lambda part: part[position], pieces))
        return jax.tree.map(lambda new, old: jnp.where(position < mine, new, old), longer, running)

    return lax.fori_loop(0, count - 1, turn, running)


def rms_apply(values, gain):
    mean_square = jnp.mean(values * values, axis=-1, keepdims=True)
    return values * lax.rsqrt(mean_square + epsilon) * gain.astype(jnp.float32)


def causal_conv(ext_vals, conv_weight, ext_ids):
    taps_count = conv_weight.shape[0]
    length = ext_vals.shape[0] - taps_count + 1
    own_ids = ext_ids[taps_count - 1 :]
    summed = jnp.zeros((length, ext_vals.shape[1]), jnp.float32)
    for offset in range(taps_count):
        window_rows = ext_vals[offset : offset + length].astype(jnp.float32)
        in_doc = (ext_ids[offset : offset + length] == own_ids)[:, None]
        summed = summed + jnp.where(in_doc, window_rows, 0.0) * conv_weight[offset].astype(
            jnp.float32
        )
    return jax.nn.silu(summed).astype(jnp.bfloat16)


def ssd_run(head_x, b_in, c_out, log_decay, step_size, doc_ids, state, last_doc, block):
    length, heads_here, channels = head_x.shape
    count = length // block

    def one_block(carry, pieces):
        state_now, prev_doc = carry
        x_blk, b_blk, c_blk, decay_blk, step_blk, ids_blk = pieces
        cumul = jnp.cumsum(decay_blk, axis=0)
        causal = jnp.arange(block)[:, None] >= jnp.arange(block)[None, :]
        in_doc = (ids_blk[:, None] == ids_blk[None, :]) & causal
        spread = jnp.where(in_doc[:, :, None], cumul[:, None, :] - cumul[None, :, :], -1e30)
        scores = jnp.dot(c_blk, b_blk.T, precision=highest)
        mixing = scores[:, :, None] * jnp.exp(spread) * step_blk[None, :, :]
        inner = jnp.einsum("tsh,shp->thp", mixing, x_blk, precision=highest)
        carried = (ids_blk == prev_doc).astype(jnp.float32)[:, None] * jnp.exp(cumul)
        outer = jnp.einsum("tn,hpn->thp", c_blk, state_now, precision=highest) * carried[:, :, None]
        to_end = jnp.where((ids_blk == ids_blk[-1])[:, None], cumul[-1][None, :] - cumul, -1e30)
        end_weight = jnp.exp(to_end) * step_blk
        fresh = jnp.einsum("sh,shp,sn->hpn", end_weight, x_blk, b_blk, precision=highest)
        keep = jnp.exp(cumul[-1]) * (ids_blk[-1] == prev_doc).astype(jnp.float32)
        state_new = state_now * keep[:, None, None] + fresh
        return ((state_new, ids_blk[-1]), inner + outer)

    pieces = (
        head_x.reshape(count, block, heads_here, channels),
        b_in.reshape(count, block, -1),
        c_out.reshape(count, block, -1),
        log_decay.reshape(count, block, heads_here),
        step_size.reshape(count, block, heads_here),
        doc_ids.reshape(count, block),
    )
    (state_end, doc_end), outputs = lax.scan(one_block, (state, last_doc), pieces)
    return (outputs.reshape(length, heads_here, channels), state_end, doc_end)


def link_states(earlier, later):
    scale_first, state_first, start_first, end_first = earlier
    scale_second, state_second, start_second, end_second = later
    joined = ((start_second == end_first) | (end_first < 0.0) | (start_second < 0.0)).astype(
        jnp.float32
    )
    passed = joined * scale_second
    return (
        passed * scale_first,
        passed[:, None, None] * state_first + state_second,
        jnp.where(start_first < 0.0, start_second, start_first),
        jnp.where(end_second < 0.0, end_first, end_second),
    )


def body(
    tokens,
    doc_ids,
    mix_gain,
    zgate_proj,
    xin_proj,
    bc_proj,
    dt_proj,
    conv_x,
    conv_bc,
    dt_bias,
    decay_rate,
    skip_gain,
    norm_gain,
    out_proj,
    moe_gain,
    router,
    routes,
    expert_gate_up,
    expert_down,
    shared_gate_up,
    shared_down,
):
    rows = tokens.shape[0]
    tp_index = lax.axis_index("tp")
    seq_count = lax.axis_size("seq")
    heads_local = dt_proj.shape[1]
    resid_in = tokens.astype(jnp.float32)
    normed_in = rms_apply(resid_in, mix_gain).astype(jnp.bfloat16)
    zgate = jnp.dot(normed_in, zgate_proj, preferred_element_type=jnp.float32).astype(jnp.bfloat16)
    x_pre = jnp.dot(normed_in, xin_proj, preferred_element_type=jnp.float32).astype(jnp.bfloat16)
    bc_pre = jnp.dot(normed_in, bc_proj, preferred_element_type=jnp.float32).astype(jnp.bfloat16)
    dt_raw = jnp.dot(normed_in, dt_proj, preferred_element_type=jnp.float32)
    tail_len = conv_x.shape[0] - 1
    marks = (doc_ids + 1).astype(jnp.bfloat16)
    prev_x, prev_bc, prev_marks = from_behind(
        (x_pre[rows - tail_len :], bc_pre[rows - tail_len :], marks[rows - tail_len :]), "seq", 1
    )
    ext_ids = jnp.concatenate([prev_marks.astype(jnp.int32) - 1, doc_ids])
    x_conv = causal_conv(jnp.concatenate([prev_x, x_pre]), conv_x, ext_ids)
    bc_conv = causal_conv(jnp.concatenate([prev_bc, bc_pre]), conv_bc, ext_ids)
    step_size = jax.nn.softplus(dt_raw + dt_bias)
    log_decay = -decay_rate * step_size
    head_x = x_conv.astype(jnp.float32).reshape(rows, heads_local, HEAD)
    b_in = bc_conv[:, :NSTATE].astype(jnp.float32)
    c_out = bc_conv[:, NSTATE:].astype(jnp.float32)
    block = 128
    start_state = jnp.zeros((heads_local, HEAD, NSTATE), jnp.float32)
    local_y, local_state, _ = ssd_run(
        head_x, b_in, c_out, log_decay, step_size, doc_ids, start_state, jnp.int32(-1), block
    )
    decay_sum = jnp.cumsum(log_decay, axis=0)
    whole_doc = (doc_ids[0] == doc_ids[-1]).astype(jnp.float32)
    element = (
        jnp.exp(decay_sum[-1]) * whole_doc,
        local_state,
        doc_ids[:1].astype(jnp.float32),
        doc_ids[-1:].astype(jnp.float32),
    )
    neutral = (
        jnp.ones((heads_local,), jnp.float32),
        jnp.zeros_like(local_state),
        jnp.full((1,), -1.0, jnp.float32),
        jnp.full((1,), -1.0, jnp.float32),
    )
    _, incoming, _, incoming_doc = prefix(element, "seq", link_states, neutral)
    carried = (doc_ids == incoming_doc[0].astype(jnp.int32)).astype(jnp.float32)[:, None] * jnp.exp(
        decay_sum
    )
    from_before = (
        jnp.einsum("tn,hpn->thp", c_out, incoming, precision=highest) * carried[:, :, None]
    )
    scanned = local_y + from_before + skip_gain[None, :, None] * head_x
    gated = scanned.reshape(rows, -1) * jax.nn.silu(zgate.astype(jnp.float32))
    square_sum = lax.psum(jnp.sum(gated * gated, axis=1), "tp")
    normed_mid = (
        gated * lax.rsqrt(square_sum[:, None] / DI + epsilon) * norm_gain.astype(jnp.float32)
    ).astype(jnp.bfloat16)
    resid = resid_in + lax.psum(
        jnp.dot(normed_mid, out_proj, preferred_element_type=jnp.float32), "tp"
    )
    moe_in = rms_apply(resid, moe_gain).astype(jnp.bfloat16)
    logits = jnp.dot(moe_in, router, preferred_element_type=jnp.float32)
    experts_all = router.shape[1]
    top_count = routes.shape[1]
    expert_iota = jnp.arange(experts_all, dtype=jnp.int32)
    picks = routes[:, :, None] == expert_iota[None, None, :]
    chosen = jnp.sum(jnp.where(picks, logits[:, None, :], 0.0), axis=2)
    sigmas = jax.nn.sigmoid(chosen)
    flat_wts = (sigmas / jnp.sum(sigmas, axis=1, keepdims=True)).reshape(-1)
    flat_routes = routes.reshape(-1)
    one_hot = (flat_routes[:, None] == expert_iota[None, :]).astype(jnp.int32)
    earlier = jnp.cumsum(one_hot, axis=0) - one_hot
    slot = jnp.sum(earlier * one_hot, axis=1)
    capacity = 2 * rows * top_count // experts_all
    experts_local = expert_down.shape[0]
    token_of = jnp.arange(rows * top_count, dtype=jnp.int32) // top_count
    dest = flat_routes * capacity + slot
    source = jnp.full((experts_all * capacity,), -1, jnp.int32).at[dest].set(token_of)
    valid = source >= 0
    send_rows = jnp.where(
        valid[:, None], moe_in[jnp.where(valid, source, 0)], jnp.zeros((), jnp.bfloat16)
    )
    send_rows = send_rows.reshape(seq_count, experts_local, capacity, D)
    both = jnp.einsum(
        "sekd,ecdf->sekcf",
        lax.all_to_all(send_rows, "seq", split_axis=0, concat_axis=0, tiled=True),
        expert_gate_up,
        preferred_element_type=jnp.float32,
    )
    act = (jax.nn.silu(both[:, :, :, 0, :]) * both[:, :, :, 1, :]).astype(jnp.bfloat16)
    partial_out = jnp.einsum(
        "sekf,efd->sekd", act, expert_down, preferred_element_type=jnp.float32
    ).astype(jnp.bfloat16)
    returned = lax.all_to_all(partial_out, "seq", split_axis=0, concat_axis=0, tiled=True)
    picked = returned.reshape(experts_all * capacity, D)[dest].astype(jnp.float32)
    moe_part = jnp.sum((picked * flat_wts[:, None]).reshape(rows, top_count, D), axis=1)
    shared_both = jnp.einsum(
        "td,cdf->tcf", moe_in, shared_gate_up, preferred_element_type=jnp.float32
    )
    shared_act = (jax.nn.silu(shared_both[:, 0, :]) * shared_both[:, 1, :]).astype(jnp.bfloat16)
    shared_part = jnp.dot(shared_act, shared_down, preferred_element_type=jnp.float32)
    added = lax.psum_scatter(moe_part + shared_part, "tp", scatter_dimension=1, tiled=True)
    resid_slice = lax.dynamic_slice_in_dim(resid, tp_index * added.shape[1], added.shape[1], 1)
    return (resid_slice + added).astype(jnp.bfloat16)


def solution(mesh):
    in_specs = (
        P("seq", None),
        P("seq"),
        P(),
        P(None, "tp"),
        P(None, "tp"),
        P(),
        P(None, "tp"),
        P(None, "tp"),
        P(),
        P("tp"),
        P("tp"),
        P("tp"),
        P("tp"),
        P("tp", None),
        P(),
        P(),
        P("seq", None),
        P("seq", None, None, "tp"),
        P("seq", "tp", None),
        P(None, None, "tp"),
        P("tp", None),
    )
    out_specs = P("seq", "tp")
    return jax.shard_map(body, mesh=mesh, in_specs=in_specs, out_specs=out_specs, check_vma=False)
```

profile of v0, /device:TPU:0, one launch (start us, length us, event | category | flops | bytes accessed | tf_op | source)
XLA Modules:
  0.0 778.7 jit_solution(14759443160048625740)
XLA Ops:
  8.0 2.1 collective-permute-start
  14.6 4.4 collective-permute-start.2
  20.6 1.9 collective-permute-start.1
  34.3 3.2 fusion.63
  40.2 49.4 %while.31 = (s32[]{:T(128)}, f32[12,64,128]{2,1,0:T(8,128)S(1)}, s32[]{:T(128)}, f32[2,128,12,64]{1,0,3,2:T(2,128)}, f32[2,128,12]{2,1,0:T(8,128)}, /*index=5*/s...) while((s32[]{:T(128)}, f32[12,64,128]{2,1,0:T(8,128)S(1)}, ...), condition=%wide.region_3.4_spmd.clone, body=%wide.region_1.3_spmd.clone.sunk | while | flops 479875968 | bytes 5811494 | solution.py:86
  54.2 10.1 %dynamic_update_slice.6 = f32[2,128,12,64]{1,0,3,2:T(2,128)} dynamic-update-slice(f32[2,128,12,64]{1,0,3,2:T(2,128)} %get-tuple-element.519, f32[1,128,12,64]{1,0,3,2:T(1,128)S(1)} %bitcast.220, s32[]{:T(128)S(6)} %copy.174, s32[]{:T(128)} %constant.107.clone.1..sunk, s32[]{:T(128)} %constant.107.clone.1..sunk, s32[]{:T(128)} %constant.107.clone.1..sunk) | dynamic-update-slice | bytes 786436 | tf_op jit(solution)/shard_map/while/body/jit(dynamic_update_index_in_dim)/dynamic_update_slice | solution.py:86
  78.9 10.1 %dynamic_update_slice.6 = f32[2,128,12,64]{1,0,3,2:T(2,128)} dynamic-update-slice(f32[2,128,12,64]{1,0,3,2:T(2,128)} %get-tuple-element.519, f32[1,128,12,64]{1,0,3,2:T(1,128)S(1)} %bitcast.220, s32[]{:T(128)S(6)} %copy.174, s32[]{:T(128)} %constant.107.clone.1..sunk, s32[]{:T(128)} %constant.107.clone.1..sunk, s32[]{:T(128)} %constant.107.clone.1..sunk) | dynamic-update-slice | bytes 786436 | tf_op jit(solution)/shard_map/while/body/jit(dynamic_update_index_in_dim)/dynamic_update_slice | solution.py:86
  99.4 65.6 %all-reduce.2 = (f32[32]{0:T(128)}, f32[32]{0:T(128)}) all-reduce(f32[32]{0:T(128)S(1)} %convert_dynamic-update-slice_fusion.1, f32[32]{0:T(128)S(1)} %convert_dynamic-update-slice_fusion), channel_id=2, replica_groups=mesh['seq'=32,'tp'=4] {'seq'}, use_global_device_ids=true, to_apply=%add | all-reduce | flops 64 | bytes 512
  165.3 19.2 %all-gather.3 = f32[32,1,12]{2,1,0:T(1,128)} all-gather(f32[1,1,12]{2,1,0:T(1,128)S(1)} %bitcast.245), channel_id=1, replica_groups=mesh['seq'=32,'tp'=4] {'seq'}, dimensions={0}, use_global_device_ids=true | all-gather | bytes 1584 | tf_op jit(solution)/shard_map/all_gather | solution.py:24
  184.5 2.6 reshape.262
  187.1 170.2 %while.32 = (s32[]{:T(128)}, f32[12,64,128]{2,1,0:T(8,128)S(1)}, f32[1]{0:T(128)}, s32[]{:T(128)}, f32[32,1]{0,1:T(1,128)}, /*index=5*/f32[32,12]{1,0:T(8,128)},...) while((s32[]{:T(128)}, f32[12,64,128]{2,1,0:T(8,128)S(1)}, ...), condition=%wide.region_7.8_spmd.clone, body=%wide.region_6.7_spmd.clone.sunk | while | flops 393241 | bytes 1180042 | solution.py:33
  358.1 2.5 fusion.47
  360.6 2.4 copy.125
  363.0 3.7 multiply_reduce_fusion.2
  366.6 11.8 %psum.14 = f32[256]{0:T(256)S(1)} all-reduce(f32[256]{0:T(256)S(1)} %get-tuple-element.377), channel_id=1, replica_groups=mesh['seq'=32,'tp'=4] {'tp'}, use_global_device_ids=true, to_apply=%region_9.10 | all-reduce | flops 256 | bytes 2048 | tf_op jit(solution)/shard_map/psum | solution.py:179
  378.5 3.1 fusion.57
  383.1 18.1 %reduce-window.16 = s32[64,12,128]{2,1,0:T(8,128)S(1)} reduce-window(s32[64,12,128]{2,1,0:T(8,128)S(1)} %fusion.54, s32[]{:T(128)} %constant.107.clone.1), window={size=1x1x128 pad=0_0x0_0x127_0}, to_apply=%region_11.12 | reduce-window | flops 12484608 | bytes 786436 | tf_op jit(solution)/shard_map/reduce-window.2
  402.3 6.2 scatter_custom_fusion
  408.6 22.5 %all-reduce.5.cloned.1.call-done = f32[256,1536]{1,0:T(8,128)} async-done(((f32[256,1536]{1,0:T(8,128)}), f32[256,1536]{1,0:T(8,128)}) %all-reduce.5.cloned.1.call-update) | async-done | bytes 1572880 | tf_op jit(solution)/shard_map/psum | solution.py:183
  433.0 14.7 %gather_fusion = bf16[3072,1536]{1,0:T(8,128)(2,1)} fusion(bf16[256,1536]{1,0:T(8,128)(2,1)S(1)} %multiply_convert_fusion, s32[3072]{0:T(1024)S(1)} %fusion.76), kind=kCustom, calls=%fused_computation | custom fusion | bytes 18886656 | tf_op jit(solution)/shard_map/gather | solution.py:206
  447.7 8.1 %broadcast_select_fusion = bf16[32,2,48,1536]{3,2,1,0:T(8,128)(2,1)} fusion(bf16[32,2,48,1536]{3,2,1,0:T(8,128)(2,1)} %bitcast.219, pred[32,2,48]{2,1,0:T(4,128)(4,1)S(1)} %broadcast_in_dim.180), kind=kLoop, calls=%fused_computation.60 | loop fusion | flops 4718592 | bytes 18877440 | tf_op jit(solution)/shard_map/jit(_where)/select_n | solution.py:205
  455.8 114.3 %all_to_all.10 = bf16[32,2,48,1536]{3,2,1,0:T(8,128)(2,1)S(1)} all-to-all(bf16[32,2,48,1536]{3,2,1,0:T(8,128)(2,1)} %broadcast_select_fusion), channel_id=1, replica_groups=mesh['seq'=32,'tp'=4] {'seq'}, dimensions={0} | all-to-all | bytes 18874368 | tf_op jit(solution)/shard_map/all_to_all | solution.py:211
  570.1 2.6 fusion.37
  572.7 5.0 convert_bitcast_fusion
  577.7 8.2 %copy.133 = bf16[32,2,48,1536]{3,2,1,0:T(8,128)(2,1)} copy(bf16[32,2,48,1536]{3,2,0,1:T(8,128)(2,1)} %convert_bitcast_fusion) | data formatting | bytes 18874368 | tf_op jit(solution)/shard_map/convert_element_type | solution.py:218
  586.0 5.1 all-to-all-start.1
  592.6 118.0 %all-to-all-done.1 = bf16[32,2,48,1536]{3,2,1,0:T(8,128)(2,1)} async-done(((bf16[32,2,48,1536]{3,2,1,0:T(8,128)(2,1)}), bf16[32,2,48,1536]{3,2,1,0:T(8,128)(2,1)}, u32[]{:S(2)}, u32[]{:S(2)}) %all-to-all-start.1) | async-done | bytes 9437216 | tf_op jit(solution)/shard_map/all_to_all | solution.py:219
  710.6 15.3 %gather_fusion.1 = bf16[1536,1536]{1,0:T(8,128)(2,1)} fusion(bf16[3072,1536]{1,0:T(8,128)(2,1)} %bitcast.33, s32[2048]{0:T(1024)S(1)} %pad_clamp_fusion), kind=kCustom, calls=%fused_computation.1 | custom fusion | bytes 9443328 | tf_op jit(solution)/shard_map/gather | solution.py:220
  725.9 8.9 %reshape.283 = f32[256,6,1536]{2,1,0:T(8,128)} reshape(bf16[1536,1536]{1,0:T(8,128)(2,1)} %gather_fusion.1) | data formatting | bytes 14155776 | tf_op jit(solution)/shard_map/convert_element_type | solution.py:220
  734.8 10.7 %multiply_reduce_fusion = f32[256,1536]{1,0:T(8,128)} fusion(f32[256,6,1536]{2,1,0:T(8,128)} %reshape.283, f32[256,6]{1,0:T(8,128)S(1)} %copy.134), kind=kLoop, calls=%fused_computation.56 | loop fusion | flops 4325376 | bytes 11016192 | tf_op jit(solution)/shard_map/reduce_sum | solution.py:221
  745.5 3.4 convolution_add_fusion.1
  748.9 21.4 %reduce-scatter.2.cloned.1.call-done = f32[256,384]{1,0:T(8,128)} async-done(((f32[256,1536]{1,0:T(8,128)}), f32[256,384]{1,0:T(8,128)}) %reduce-scatter.2.cloned.1.call-update) | async-done | bytes 393232 | tf_op jit(solution)/shard_map/reduce_scatter | solution.py:227
  (286 shorter events, 160.7 us)
Async XLA Ops:
  6.5 371.9 %copy-start = (bf16[768,1536]{1,0:T(8,128)(2,1)S(1)}, bf16[768,1536]{1,0:T(8,128)(2,1)}, u32[]{:S(2)}) copy-start(bf16[768,1536]{1,0:T(8,128)(2,1)} %param.38) | copy-start | bytes 7077892
  6.5 180.6 %all-gather.6.cloned.1.call-start = ((), (), s32[]{:S(2)}) async-start(), calls=%async_computation.5 | async-start | bytes 12976128 | tf_op jit(solution)/shard_map/all_gather | solution.py:24
  8.0 11.0 %copy-start.7 = (bf16[256,1536]{1,0:T(8,128)(2,1)S(1)}, bf16[256,1536]{1,0:T(8,128)(2,1)}, u32[]{:S(2)}) copy-start(bf16[256,1536]{1,0:T(8,128)(2,1)} %param.25) | copy-start | bytes 2359300
  8.0 11.0 %copy-start.29 = (bf16[1536,768]{1,0:T(8,128)(2,1)S(1)}, bf16[1536,768]{1,0:T(8,128)(2,1)}, u32[]{:S(2)}) copy-start(bf16[1536,768]{1,0:T(8,128)(2,1)} %param.29) | copy-start | bytes 7077892
  8.0 22.1 %collective-permute-start = (bf16[3]{0:T(256)(128)(2,1)}, bf16[3]{0:T(256)(128)(2,1)}, u32[]{:S(2)}, u32[]{:S(2)}) collective-permute-start(bf16[3]{0:T(256)(128)(2,1)} %slice.114), channel_id=1, source_target_pairs={{0,4},{4,8},{8,12},{12,16},{16,20},{20,24},{24,28},{28,32},{32,36}... | collective-permute-start | bytes 26 | tf_op jit(solution)/shard_map/ppermute | solution.py:19
  11.5 8.4 %copy-start.26 = (f32[256]{0:T(256)}, f32[256]{0:T(256)S(1)}, u32[]{:S(2)}) copy-start(f32[256]{0:T(256)S(1)} %add_rsqrt_fusion.2) | copy-start | bytes 3076
  12.2 6.8 copy-start.23
  14.6 10.0 %copy-start.20 = (bf16[4,768]{1,0:T(4,128)(2,1)S(1)}, bf16[4,768]{1,0:T(4,128)(2,1)}, u32[]{:S(2)}) copy-start(bf16[4,768]{1,0:T(4,128)(2,1)} %param.32) | copy-start | bytes 18436
  14.6 16.3 %collective-permute-start.2 = (bf16[3,256]{1,0:T(4,128)(2,1)}, bf16[3,256]{1,0:T(4,128)(2,1)}, u32[]{:S(2)}, u32[]{:S(2)}) collective-permute-start(bf16[3,256]{1,0:T(4,128)(2,1)} %slice.159), channel_id=1, source_target_pairs={{0,4},{4,8},{8,12},{12,16},{16,20},{20,24},{24,28},{28,32},{32,36}... | collective-permute-start | bytes 4616 | tf_op jit(solution)/shard_map/ppermute | solution.py:19
  19.9 10.9 %copy-start.17 = (s32[256]{0:T(256)S(1)}, s32[256]{0:T(256)}, u32[]{:S(2)}) copy-start(s32[256]{0:T(256)} %param.26) | copy-start | bytes 3076
  20.6 13.7 %collective-permute-start.1 = (bf16[3,768]{1,0:T(4,128)(2,1)}, bf16[3,768]{1,0:T(4,128)(2,1)}, u32[]{:S(2)}, u32[]{:S(2)}) collective-permute-start(bf16[3,768]{1,0:T(4,128)(2,1)} %slice.154), channel_id=1, source_target_pairs={{0,4},{4,8},{8,12},{12,16},{16,20},{20,24},{24,28},{28,32},{32,36}... | collective-permute-start | bytes 13832 | tf_op jit(solution)/shard_map/ppermute | solution.py:19
  23.2 3.9 copy-start.28
  25.3 9.0 %copy-start.21 = (f32[768]{0:T(1024)S(1)}, f32[768]{0:T(1024)}, u32[]{:S(2)}) copy-start(f32[768]{0:T(1024)} %get-tuple-element.313) | copy-start | bytes 9220
  25.3 9.0 %copy-start.22 = (f32[768]{0:T(1024)S(1)}, f32[768]{0:T(1024)}, u32[]{:S(2)}) copy-start(f32[768]{0:T(1024)} %get-tuple-element.314) | copy-start | bytes 9220
  48.7 4.8 copy-start.6
  53.5 10.8 %copy-start.18 = (s32[256]{0:T(256)S(1)}, s32[256]{0:T(256)}, u32[]{:S(2)}) copy-start(s32[256]{0:T(256)} %get-tuple-element.602) | copy-start | bytes 3076 | tf_op jit(solution)/shard_map/while
  73.4 4.8 copy-start.6
  78.2 10.8 %copy-start.18 = (s32[256]{0:T(256)S(1)}, s32[256]{0:T(256)}, u32[]{:S(2)}) copy-start(s32[256]{0:T(256)} %get-tuple-element.602) | copy-start | bytes 3076 | tf_op jit(solution)/shard_map/while
  90.4 340.6 %all-reduce.5.cloned.1.call-start = ((), (), s32[]{:S(2)}) async-start(), calls=%async_computation.3 | async-start | bytes 3145728 | tf_op jit(solution)/shard_map/psum | solution.py:183
  187.1 170.9 %copy-start.5 = (f32[256,768]{0,1:T(8,128)S(1)}, f32[256,768]{0,1:T(8,128)}, u32[]{:S(2)}) copy-start(f32[256,768]{0,1:T(8,128)} %copy-done.4) | copy-start | bytes 2359300
  358.1 4.9 copy-start.24
  358.1 4.9 copy-start.27
  360.6 2.4 copy-start.8
  363.0 15.5 %copy-start.19 = (f32[768]{0:T(1024)S(1)}, f32[768]{0:T(1024)}, u32[]{:S(2)}) copy-start(f32[768]{0:T(1024)} %convert_element_type.182) | copy-start | bytes 9220
  432.7 14.9 %copy-start.3 = (f32[256,1536]{1,0:T(8,128)}, f32[256,1536]{1,0:T(8,128)S(1)}, u32[]{:S(2)}) copy-start(f32[256,1536]{1,0:T(8,128)S(1)} %get-tuple-element.359) | copy-start | bytes 4718596
  455.7 114.3 %copy-start.30 = (bf16[2,2,1536,128]{3,2,1,0:T(8,128)(2,1)S(1)}, bf16[2,2,1536,128]{3,2,1,0:T(8,128)(2,1)}, u32[]{:S(2)}) copy-start(bf16[2,2,1536,128]{3,2,1,0:T(8,128)(2,1)} %param.42) | copy-start | bytes 4718596
  570.1 2.6 copy-start.11
  586.0 5.4 copy-start.13
  586.0 6.0 copy-start.9
  586.0 124.6 %all-to-all-start.1 = ((bf16[32,2,48,1536]{3,2,1,0:T(8,128)(2,1)}), bf16[32,2,48,1536]{3,2,1,0:T(8,128)(2,1)}, u32[]{:S(2)}, u32[]{:S(2)}) async-start(bf16[32,2,48,1536]{3,2,1,0:T(8,128)(2,1)} %copy.133), calls=%async_computation.1 | async-start | bytes 18874368 | tf_op jit(solution)/shard_map/all_to_all | solution.py:219
  591.1 179.3 %reduce-scatter.2.cloned.1.call-start = ((), (), s32[]{:S(2)}) async-start(), calls=%async_computation.4 | async-start | bytes 1966080 | tf_op jit(solution)/shard_map/reduce_scatter | solution.py:227
  745.5 26.7 %copy-start.1 = (bf16[768,1536]{1,0:T(8,128)(2,1)S(1)}, bf16[768,1536]{1,0:T(8,128)(2,1)}, u32[]{:S(2)}) copy-start(bf16[768,1536]{1,0:T(8,128)(2,1)} %param.38) | copy-start | bytes 7077892
  (9 other events, 8.4 us)
Sparse Core Ops, SparseCore 0:
  90.5 65.3 all-gather.5
  381.7 49.2 all-reduce.4
  749.0 21.2 reduce-scatter.1
where the time goes:
time: 786 us; the launch traced here: 779 us
  blocking collectives  211 us (27%)
  waiting for transfers between devices  162 us (21%)
  local copies, waits for them, and re-layouts  139 us (18%)
  other arithmetic  125 us (16%)
  loops' own time  77.8 us (10%)
  matrix products  35.4 us (5%)
  between operations  14.8 us (2%)
  starting transfers between devices  13.9 us (2%)
    all_to_all x1, waiting for transfers between devices, body(): lax.all_to_all(partial_out, 'seq', split_axis=0, concat_axis=0, tiled=True)  118 us
    all_to_all x1, blocking collectives, body(): lax.all_to_all(send_rows, 'seq', split_axis=0, concat_axis=0, tiled=True)  114 us
    another operation x1, loops' own time, prefix(): return lax.fori_loop(0, count - 1, turn, running)  75.1 us
    unnamed x1, blocking collectives  65.6 us
    dynamic_slice x31, local copies, waits for them, and re-layouts, turn(): longer = join(running, jax.tree.map(lambda part: part[position], pieces))  39.4 us
    select_n x31, other arithmetic, turn(): jnp.where(position < mine, new, old)  34.4 us
    psum x1, waiting for transfers between devices, body(): lax.psum(jnp.dot(normed_mid, out_proj, preferred_element_type=jnp.float32...  22.5 us
    reduce_scatter x1, waiting for transfers between devices, body(): lax.psum_scatter(moe_part + shared_part, 'tp', scatter_dimension=1, tiled...  21.4 us
  transfers between devices with their start and end apart: 7, of which 3 were waited for; matrix products, arithmetic and copies ran while one was open for 7% of the time, Pallas kernels for 0%

commit v1 on v0

v1 whole, which is shorter than its diff:
```python
import functools

import jax
import jax.numpy as jnp
from jax import lax
from jax.experimental import pallas as pl
from jax.experimental.pallas import tpu as pltpu
from jax.sharding import PartitionSpec as P

D = 1536
HEAD = 64
NSTATE = 128
DI = 3072
epsilon = 1e-05
highest = lax.Precision.HIGHEST
F32 = jnp.float32
BF = jnp.bfloat16


def rms_apply(values, gain):
    mean_square = jnp.mean(values * values, axis=-1, keepdims=True)
    return values * lax.rsqrt(mean_square + epsilon) * gain.astype(F32)


def silu(v):
    return v / (1.0 + jnp.exp(-v))


def mixer_kernel(
    heads, xe_ref, be_ref, ids_ref, idrow_ref, dt_ref, rate_ref, cx_ref, cb_ref, skip_ref,
    y_ref, st_ref, c_ref, car_ref, tot_ref, xs_ref, bs_ref,
):
    n = y_ref.shape[0]
    width = y_ref.shape[1]
    xs_ref[...] = xe_ref[...].astype(F32)
    bs_ref[...] = be_ref[...].astype(F32)
    own = ids_ref[pl.ds(8, n), :]
    xsum = jnp.zeros((n, width), F32)
    bsum = jnp.zeros((n, 2 * NSTATE), F32)
    for k in range(4):
        live = ids_ref[pl.ds(5 + k, n), :] == own
        xsum += jnp.where(live, xs_ref[pl.ds(5 + k, n), :], 0.0) * cx_ref[k : k + 1, :]
        bsum += jnp.where(live, bs_ref[pl.ds(5 + k, n), :], 0.0) * cb_ref[k : k + 1, :]
    x_conv = silu(xsum).astype(BF).astype(F32)
    bc = silu(bsum).astype(BF)
    b_in, c_out = bc[:, :NSTATE], bc[:, NSTATE:]
    c_ref[...] = c_out
    raw = dt_ref[...]
    step = jnp.maximum(raw, 0.0) + jnp.log1p(jnp.exp(-jnp.abs(raw)))
    decay = -rate_ref[...] * step
    row = lax.broadcasted_iota(jnp.int32, (n, n), 0)
    col = lax.broadcasted_iota(jnp.int32, (n, n), 1)
    causal = row >= col
    tri = jnp.where(causal, 1.0, 0.0)
    cum = jnp.dot(tri, decay, precision=highest, preferred_element_type=F32)
    cum_t = cum.T
    last = cum[n - 1 : n, :]
    tot_ref[...] = last
    expand = jnp.where(
        lax.broadcasted_iota(jnp.int32, (128, width), 1) // HEAD
        == lax.broadcasted_iota(jnp.int32, (128, width), 0),
        1.0,
        0.0,
    )
    step_w = jnp.dot(step, expand, precision=highest, preferred_element_type=F32)
    at_end = own == ids_ref[n + 7 : n + 8, :]
    to_end = jnp.where(at_end, jnp.exp(last - cum), 0.0)
    end_w = jnp.dot(to_end, expand, precision=highest, preferred_element_type=F32)
    car_ref[...] = jnp.dot(jnp.exp(cum), expand, precision=highest, preferred_element_type=F32)
    x_step = x_conv * step_w
    x_in = x_step.astype(BF)
    st_ref[...] = lax.dot_general(
        b_in, (x_step * end_w).astype(BF), (((0,), (0,)), ((), ())), preferred_element_type=F32
    )
    scores = lax.dot_general(c_out, b_in, (((1,), (1,)), ((), ())), preferred_element_type=F32)
    scores = jnp.where(causal & (own == idrow_ref[...]), scores, 0.0)
    skip = x_conv * skip_ref[...]
    half = n // 2
    for top, bottom in ((0, half), (half, n)):
        for pair in range(heads // 2):
            parts = []
            for h in (2 * pair, 2 * pair + 1):
                diff = cum[top:bottom, h : h + 1] - cum_t[h : h + 1, :bottom]
                mixing = (scores[top:bottom, :bottom] * jnp.exp(jnp.minimum(diff, 0.0))).astype(BF)
                parts.append(
                    jnp.dot(
                        mixing, x_in[:bottom, h * HEAD : (h + 1) * HEAD], preferred_element_type=F32
                    )
                )
            cols = slice(pair * 128, pair * 128 + 128)
            y_ref[top:bottom, cols] = jnp.concatenate(parts, axis=1) + skip[top:bottom, cols]


def mixer_local(x_ext, bc_ext, ids_ext, ids_row, dt, rate, conv_x, conv_bc, skip, heads):
    n, width = x_ext.shape[0] - 8, x_ext.shape[1]
    vm = pl.BlockSpec(memory_space=pltpu.VMEM)
    return pl.pallas_call(
        functools.partial(mixer_kernel, heads),
        out_shape=(
            jax.ShapeDtypeStruct((n, width), F32),
            jax.ShapeDtypeStruct((NSTATE, width), F32),
            jax.ShapeDtypeStruct((n, NSTATE), BF),
            jax.ShapeDtypeStruct((n, width), F32),
            jax.ShapeDtypeStruct((1, 128), F32),
        ),
        in_specs=[vm] * 9,
        out_specs=(vm,) * 5,
        scratch_shapes=[pltpu.VMEM((n + 8, width), F32), pltpu.VMEM((n + 8, 2 * NSTATE), F32)],
        name="mixer_local",
    )(x_ext, bc_ext, ids_ext, ids_row, dt, rate, conv_x, conv_bc, skip)


def expert_kernel(x_ref, w_ref, gu_hbm, dn_hbm, o_ref, gu, dn, sem):
    parts, experts = gu_hbm.shape[0], gu_hbm.shape[1]
    wide = gu_hbm.shape[4]

    def copies():
        out = []
        for t in range(parts):
            for e in range(experts):
                for c in range(2):
                    out.append(
                        pltpu.make_async_copy(
                            gu_hbm.at[t, e, c],
                            gu.at[e, :, pl.ds((c * parts + t) * wide, wide)],
                            sem.at[len(out)],
                        )
                    )
                out.append(
                    pltpu.make_async_copy(
                        dn_hbm.at[t, e], dn.at[e, pl.ds(t * wide, wide), :], sem.at[len(out)]
                    )
                )
        return out

    @pl.when(pl.program_id(0) == 0)
    def _():
        for copy in copies():
            copy.start()
        for copy in copies():
            copy.wait()

    x = x_ref[...]
    total = None
    hidden = parts * wide
    for e in range(experts):
        both = jnp.dot(x, gu[e], preferred_element_type=F32)
        act = (silu(both[:, :hidden]) * both[:, hidden:] * w_ref[:, e : e + 1]).astype(BF)
        out = jnp.dot(act, dn[e], preferred_element_type=F32)
        total = out if total is None else total + out
    o_ref[...] = total.astype(BF)


def experts_dense(x, wts, gate_up, down):
    rows = x.shape[0]
    parts, experts, _, _, wide = gate_up.shape
    tile = 256
    hidden = parts * wide
    return pl.pallas_call(
        expert_kernel,
        out_shape=jax.ShapeDtypeStruct((rows, D), BF),
        grid=(rows // tile,),
        in_specs=[
            pl.BlockSpec((tile, D), lambda i: (i, 0)),
            pl.BlockSpec((tile, experts), lambda i: (i, 0)),
            pl.BlockSpec(memory_space=pl.ANY),
            pl.BlockSpec(memory_space=pl.ANY),
        ],
        out_specs=pl.BlockSpec((tile, D), lambda i: (i, 0)),
        scratch_shapes=[
            pltpu.VMEM((experts, D, 2 * hidden), BF),
            pltpu.VMEM((experts, hidden, D), BF),
            pltpu.SemaphoreType.DMA((parts * experts * 3,)),
        ],
        compiler_params=pltpu.CompilerParams(vmem_limit_bytes=40 << 20),
        name="experts_dense",
    )(x, wts, gate_up, down)


def body(
    tokens, doc_ids, mix_gain, zgate_proj, xin_proj, bc_proj, dt_proj, conv_x, conv_bc, dt_bias,
    decay_rate, skip_gain, norm_gain, out_proj, moe_gain, router, routes, expert_gate_up,
    expert_down, shared_gate_up, shared_down,
):
    rows = tokens.shape[0]
    tp_index, seq_index = lax.axis_index("tp"), lax.axis_index("seq")
    tp_count, seq_count = lax.axis_size("tp"), lax.axis_size("seq")
    heads = dt_proj.shape[1]
    width = heads * HEAD
    part = rows // tp_count
    experts_local = expert_down.shape[0]

    gate_up_all = lax.all_gather(expert_gate_up, "tp")
    down_all = lax.all_gather(expert_down, "tp")
    own_routes = lax.dynamic_slice_in_dim(routes, tp_index * part, part, 0)
    plane_routes = lax.all_gather(own_routes, "seq", tiled=True)

    resid_in = tokens.astype(F32)
    normed_in = rms_apply(resid_in, mix_gain).astype(BF)
    zgate = jnp.dot(normed_in, zgate_proj, preferred_element_type=F32).astype(BF)
    x_pre = jnp.dot(normed_in, xin_proj, preferred_element_type=F32).astype(BF)
    bc_pre = jnp.dot(normed_in, bc_proj, preferred_element_type=F32).astype(BF)
    dt_raw = jnp.dot(normed_in, dt_proj, preferred_element_type=F32) + dt_bias
    dt_raw = jnp.pad(dt_raw, ((0, 0), (0, 128 - heads)))
    rate = jnp.pad(decay_rate, (0, 128 - heads))[None, :]
    marks = jnp.broadcast_to((doc_ids[-8:, None] + 1).astype(BF), (8, 128))
    tail = jnp.concatenate([x_pre[-8:], bc_pre[-8:], marks], axis=1)
    prev = lax.ppermute(tail, "seq", [(s, s + 1) for s in range(seq_count - 1)])
    prev_ids = prev[:, width + 256].astype(jnp.int32) - 1
    ids_ext = jnp.concatenate([prev_ids, doc_ids])
    x_ext = jnp.concatenate([prev[:, :width], x_pre])
    bc_ext = jnp.concatenate([prev[:, width : width + 256], bc_pre])
    local_y, state, c_out, carry_w, total = mixer_local(
        x_ext, bc_ext, ids_ext[:, None], doc_ids[None, :], dt_raw, rate,
        conv_x.astype(F32), conv_bc.astype(F32), jnp.repeat(skip_gain, HEAD)[None, :], heads,
    )

    note = jnp.concatenate([total[0, :heads], doc_ids[-1:].astype(F32)])
    notes = lax.all_gather(note, "seq")
    ends = notes[:, heads]
    gone = jnp.cumsum(notes[:, :heads], axis=0)
    ends_before = jnp.concatenate([jnp.full((1,), -1.0, F32), ends[:-1]])
    gone_before = jnp.concatenate([jnp.zeros((1, heads), F32), gone[:-1]])
    index = jnp.arange(seq_count)
    reach = (index[None, :] < index[:, None]) & (ends[None, :] == ends_before[:, None])
    link = jnp.where(
        reach[:, :, None],
        jnp.exp(jnp.minimum(gone_before[:, None, :] - gone[None, :, :], 0.0)),
        0.0,
    )
    share = state.reshape(seq_count, NSTATE // seq_count, width)
    share = lax.all_to_all(share, "seq", split_axis=0, concat_axis=0, tiled=True)
    share = share.reshape(seq_count, NSTATE // seq_count, heads, HEAD)
    share = jnp.einsum("qsh,snhp->qnhp", link, share, precision=highest)
    share = share.reshape(seq_count, NSTATE // seq_count, width)
    incoming = lax.all_to_all(share, "seq", split_axis=0, concat_axis=0, tiled=True)
    incoming = incoming.reshape(NSTATE, width)
    before = jnp.dot(c_out, incoming.astype(BF), preferred_element_type=F32)
    carried = doc_ids.astype(F32) == ends_before[seq_index]
    scanned = local_y + jnp.where(carried[:, None], before * carry_w, 0.0)
    gated = scanned * jax.nn.silu(zgate.astype(F32))
    squares = jnp.sum(gated * gated, axis=1)
    inner = (gated * norm_gain.astype(F32)).astype(BF)
    projected = jnp.dot(inner, out_proj, preferred_element_type=F32)
    squares = lax.psum_scatter(squares, "tp", tiled=True)
    projected = lax.psum_scatter(projected, "tp", scatter_dimension=0, tiled=True)
    own_rows = lax.dynamic_slice_in_dim(resid_in, tp_index * part, part, 0)
    resid = own_rows + projected * lax.rsqrt(squares[:, None] / DI + epsilon)
    moe_in = rms_apply(resid, moe_gain).astype(BF)

    plane = lax.all_gather(moe_in, "seq", tiled=True)
    line = lax.all_gather(moe_in, "tp", tiled=True)
    logits = jnp.dot(plane, router, preferred_element_type=F32)
    iota = jnp.arange(router.shape[1], dtype=jnp.int32)
    named = jnp.any(plane_routes[:, :, None] == iota[None, None, :], axis=1)
    sigmas = jnp.where(named, jax.nn.sigmoid(logits), 0.0)
    wts = sigmas / jnp.sum(sigmas, axis=1, keepdims=True)
    wts = lax.dynamic_slice_in_dim(wts, seq_index * experts_local, experts_local, 1)
    routed = experts_dense(plane, wts, gate_up_all, down_all)
    routed = lax.psum_scatter(routed, "seq", scatter_dimension=0, tiled=True)
    shared_gate = jnp.dot(line, shared_gate_up[0], preferred_element_type=F32)
    shared_up = jnp.dot(line, shared_gate_up[1], preferred_element_type=F32)
    shared_act = (jax.nn.silu(shared_gate) * shared_up).astype(BF)
    shared_part = jnp.dot(shared_act, shared_down, preferred_element_type=F32)
    mine = lax.dynamic_slice_in_dim(shared_part, tp_index * part, part, 0)
    whole = lax.dynamic_update_slice_in_dim(
        shared_part, mine + resid + routed.astype(F32), tp_index * part, 0
    )
    added = lax.psum_scatter(whole, "tp", scatter_dimension=1, tiled=True)
    return added.astype(BF)


def solution(mesh):
    in_specs = (
        P("seq", None), P("seq"), P(), P(None, "tp"), P(None, "tp"), P(), P(None, "tp"),
        P(None, "tp"), P(), P("tp"), P("tp"), P("tp"), P("tp"), P("tp", None), P(), P(),
        P("seq", None), P("seq", None, None, "tp"), P("seq", "tp", None), P(None, None, "tp"),
        P("tp", None),
    )
    return jax.shard_map(
        body, mesh=mesh, in_specs=in_specs, out_specs=P("seq", "tp"), check_vma=False
    )
```

time: 786 us -> 475 us (0.60)
  local copies, waits for them, and re-layouts: 139 us -> 19.1 us
  other arithmetic: 125 us -> 16 us
  blocking collectives: 211 us -> 118 us
  waiting for transfers between devices: 162 us -> 243 us
  loops' own time: 77.8 us -> 0 us
  Pallas kernels: 0 us -> 31.3 us
  matrix products: 35.4 us -> 21.9 us
    all_gather x1 -> x3, waiting for transfers between devices: 0.01 us -> 124 us  [the longest x1 67.4 us: body(): gate_up_all = lax.all_gather(expert_gate_up, 'tp')]
    all_to_all x1 -> x0, blocking collectives: 114 us -> none  [body(): lax.all_to_all(send_rows, 'seq', split_axis=0, concat_axis=0, tiled=True)]
    all_to_all x1 -> x2, waiting for transfers between devices: 118 us -> 15.8 us  [body(): lax.all_to_all(share, 'seq', split_axis=0, concat_axis=0, tiled=True)]
    reduce_scatter x1 -> x3, waiting for transfers between devices: 21.4 us -> 102 us  [the longest x1 65.9 us: body(): routed = lax.psum_scatter(routed, 'seq', scatter_dimension=0, tiled=True)]
    another operation x2 -> x0, loops' own time: 77.8 us -> none  [the longest x1 75.1 us: prefix(): return lax.fori_loop(0, count - 1, turn, running)]
    select_n x34 -> x0, other arithmetic: 42.5 us -> none  [the longest x31 34.4 us: turn(): jnp.where(position < mine, new, old)]
    dynamic_slice x33 -> x1, local copies, waits for them, and re-layouts: 42.4 us -> 0.65 us  [body(): carried = doc_ids.astype(F32) == ends_before[seq_index]]
    pallas_call x0 -> x2, Pallas kernels: none -> 31.3 us  [the longest x1 26.1 us: experts_dense(): pl.pallas_call(expert_kernel, out_shape=jax.ShapeDtypeStruct((rows, D), B...]
  transfers between devices with their start and end apart: 7 -> 9, of which waited for: 3 -> 8; matrix products, arithmetic and copies ran while one was open for 7% -> 5% of each run, Pallas kernels for 0% -> 0%
where the time goes in v1:
time: 475 us; the launch traced here: 474 us
  waiting for transfers between devices  243 us (51%)
  blocking collectives  118 us (25%)
  Pallas kernels  31.3 us (7%)
  matrix products  21.9 us (5%)
  local copies, waits for them, and re-layouts  19.1 us (4%)
  other arithmetic  16 us (3%)
  between operations  15.2 us (3%)
  starting transfers between devices  9.98 us (2%)
    unnamed x2, blocking collectives  79.5 us
    all_gather x1, waiting for transfers between devices, body(): gate_up_all = lax.all_gather(expert_gate_up, 'tp')  67.4 us
    reduce_scatter x1, waiting for transfers between devices, body(): routed = lax.psum_scatter(routed, 'seq', scatter_dimension=0, tiled=True)  65.9 us
    all_gather x1, waiting for transfers between devices, body(): down_all = lax.all_gather(expert_down, 'tp')  35 us
    pallas_call x1, Pallas kernels, experts_dense(): pl.pallas_call(expert_kernel, out_shape=jax.ShapeDtypeStruct((rows, D), B...  26.1 us
    reduce_scatter x1, waiting for transfers between devices, body(): added = lax.psum_scatter(whole, 'tp', scatter_dimension=1, tiled=True)  25.6 us
    all_gather x1, blocking collectives, body(): plane_routes = lax.all_gather(own_routes, 'seq', tiled=True)  24.7 us
    all_gather x1, waiting for transfers between devices, body(): plane = lax.all_gather(moe_in, 'seq', tiled=True)  21.4 us
  transfers between devices with their start and end apart: 9, of which 8 were waited for; matrix products, arithmetic and copies ran while one was open for 5% of the time, Pallas kernels for 0%

profile of v1, /device:TPU:0, one launch (start us, length us, event | category | flops | bytes accessed | tf_op | source)
XLA Modules:
  0.0 474.3 jit_solution(16459761848496550523)
XLA Ops:
  7.4 1.4 multiply_reduce_fusion
  8.8 2.9 convolution_convert_fusion.1
  21.6 5.3 %mixer_local.1 = (f32[256,768]{1,0:T(8,128)}, f32[128,768]{1,0:T(8,128)}, bf16[256,128]{1,0:T(8,128)(2,1)}, f32[256,768]{1,0:T(8,128)}, f32[1,128]{1,0:T(1,128)}) custom-call(bf16[264,768]{1,0:T(8,128)(2,1)} %pad_maximum_fusion.xe_ref, bf16[264,256]{1,0:T(8,128)(2,1)} %pad_maximum_fusion.1.be_ref, s32[264,1]{1,0:T(8,128)} %broadcast_in_dim.70.ids_ref, ...), custom_call_target="tpu_custom_call" | custom-call | tf_op jit(solution)/shard_map/mixer_local/pallas_call | solution.py:97
  28.2 67.4 %all-reduce.3 = f32[416]{0:T(512)S(1)} all-reduce(f32[416]{0:T(512)S(1)} %maximum_dynamic-update-slice_fusion), channel_id=2, replica_groups=mesh['seq'=32,'tp'=4] {'seq'}, use_global_device_ids=true, to_apply=%add.3 | all-reduce | flops 416 | bytes 3328
  95.9 1.9 reshape.89
  97.7 4.6 all-to-all-start
  103.6 8.9 %all-to-all-done = f32[32,4,768]{2,1,0:T(4,128)} async-done(((f32[32,4,768]{2,1,0:T(4,128)}), f32[32,4,768]{2,1,0:T(4,128)}, u32[]{:S(2)}, u32[]{:S(2)}) %all-to-all-start) | async-done | bytes 393248 | tf_op jit(solution)/shard_map/all_to_all | solution.py:232
  113.9 1.4 convolution_bitcast_fusion
  116.3 2.0 reshape.104
  118.3 3.9 all-to-all-start.1
  123.5 6.9 %all-to-all-done.1 = bf16[32,4,768]{2,1,0:T(4,128)(2,1)S(1)} async-done(((bf16[32,4,768]{2,1,0:T(4,128)(2,1)}), bf16[32,4,768]{2,1,0:T(4,128)(2,1)S(1)}, u32[]{:S(2)}, u32[]{:S(2)}) %all-to-all-start.1) | async-done | bytes 196640 | tf_op jit(solution)/shard_map/all_to_all | solution.py:236
  131.5 3.1 multiply_reduce_fusion.1
  134.7 1.9 fusion.16
  136.7 1.3 convert_element_type.72
  139.3 12.1 %all-reduce.4 = f32[256]{0:T(256)S(1)} all-reduce(f32[256]{0:T(256)S(1)} %get-tuple-element.17), channel_id=6, replica_groups=mesh['seq'=32,'tp'=4] {'tp'}, use_global_device_ids=true, to_apply=%region_4.5.clone | all-reduce | flops 256 | bytes 2048
  151.5 10.3 %reduce-scatter.4.cloned.1.call-done = f32[64,1536]{1,0:T(8,128)} async-done(((f32[256,1536]{1,0:T(8,128)}), f32[64,1536]{1,0:T(8,128)}) %reduce-scatter.4.cloned.1.call-update) | async-done | bytes 393232 | tf_op jit(solution)/shard_map/reduce_scatter | solution.py:246
  161.8 1.3 multiply_reduce_fusion.2
  166.2 24.7 %all-gather.3 = s32[32,64,6]{1,2,0:T(8,128)S(1)} all-gather(s32[1,64,6]{1,2,0:T(8,128)S(1)} %dynamic-slice_bitcast_fusion), channel_id=1, replica_groups=mesh['seq'=32,'tp'=4] {'seq'}, dimensions={0}, use_global_device_ids=true | all-gather | bytes 50688 | tf_op jit(solution)/shard_map/all_gather | solution.py:196
  191.8 21.4 %all-gather.8.cloned.1.call-done.x_ref = bf16[2048,1536]{1,0:T(8,128)(2,1)} async-done(((bf16[64,1536]{1,0:T(8,128)(2,1)}), bf16[2048,1536]{1,0:T(8,128)(2,1)}) %all-gather.8.cloned.1.call-update) | async-done | bytes 6291472 | tf_op jit(solution)/shard_map/all_gather | solution.py:251
  213.2 4.7 fusion.38
  218.5 35.0 %all-gather.12.cloned.1.call-done = bf16[8,128,1536]{2,1,0:T(8,128)(2,1)} async-done(((bf16[2,128,1536]{2,1,0:T(8,128)(2,1)}), bf16[8,128,1536]{2,1,0:T(8,128)(2,1)}) %all-gather.12.cloned.1.call-update) | async-done | bytes 3145744 | tf_op jit(solution)/shard_map/all_gather | solution.py:194
  253.4 67.4 %all-gather.10.cloned.1.call-done = bf16[8,2,1536,128]{3,2,1,0:T(8,128)(2,1)} async-done(((bf16[2,2,1536,128]{3,2,1,0:T(8,128)(2,1)}), bf16[8,2,1536,128]{3,2,1,0:T(8,128)(2,1)}) %all-gather.10.cloned.1.call-update) | async-done | bytes 6291472 | tf_op jit(solution)/shard_map/all_gather | solution.py:193
  320.9 1.9 copy-done.2
  322.8 26.1 %experts_dense.1 = bf16[2048,1536]{1,0:T(8,128)(2,1)S(1)} custom-call(bf16[2048,1536]{1,0:T(8,128)(2,1)} %all-gather.8.cloned.1.call-done.x_ref, f32[2048,2]{1,0:T(8,128)S(1)} %dynamic-slice_divide_fusion.w_ref, bf16[4,2,2,1536,128]{4,3,2,1,0:T(8,128)(2,1)} %bitcast.43, bf16[4,2,128,1536]{3,2,1,0:T(8,128)(2,1)S(1)} %bitcast.42), custom_call_target="tpu_custom_call" | custom-call | tf_op jit(solution)/shard_map/experts_dense/pallas_call | solution.py:159
  348.9 2.7 copy-done.1
  352.4 14.0 %all_gather.29 = bf16[256,1536]{1,0:T(8,128)(2,1)S(1)} all-gather(bf16[64,1536]{1,0:T(8,128)(2,1)S(1)} %copy-done.7), channel_id=1, replica_groups=mesh['seq'=32,'tp'=4] {'tp'}, dimensions={0}, use_global_device_ids=true | all-gather | bytes 983040 | tf_op jit(solution)/shard_map/all_gather | solution.py:252
  366.4 2.2 fusion.10
  368.6 3.7 fusion.7
  372.4 65.9 %reduce-scatter.6.cloned.1.call-done = bf16[64,1536]{1,0:T(8,128)(2,1)} async-done(((bf16[2048,1536]{1,0:T(8,128)(2,1)}), bf16[64,1536]{1,0:T(8,128)(2,1)}) %reduce-scatter.6.cloned.1.call-update) | async-done | bytes 196624 | tf_op jit(solution)/shard_map/reduce_scatter | solution.py:260
  438.3 1.8 add_dynamic-update-slice_fusion
  440.2 25.6 %reduce-scatter.8.cloned.1.call-done = f32[256,384]{1,0:T(8,128)} async-done(((f32[256,1536]{1,0:T(8,128)}), f32[256,384]{1,0:T(8,128)}) %reduce-scatter.8.cloned.1.call-update) | async-done | bytes 393232 | tf_op jit(solution)/shard_map/reduce_scatter | solution.py:269
  465.8 1.7 convert_element_type.93
  (114 shorter events, 23.8 us)
Async XLA Ops:
  6.5 128.1 %copy-start = (bf16[768,1536]{1,0:T(8,128)(2,1)S(1)}, bf16[768,1536]{1,0:T(8,128)(2,1)}, u32[]{:S(2)}) copy-start(bf16[768,1536]{1,0:T(8,128)(2,1)} %param.34) | copy-start | bytes 7077892
  8.8 5.0 %copy-start.15 = (f32[256]{0:T(256)}, f32[256]{0:T(256)S(1)}, u32[]{:S(2)}) copy-start(f32[256]{0:T(256)S(1)} %add_rsqrt_fusion) | copy-start | bytes 3076
  8.8 2.9 copy-start.5
  8.8 2.9 copy-start.17
  11.7 2.1 copy-start.19
  11.7 2.1 copy-start.20
  11.7 2.5 copy-start.21
  11.7 3.6 copy-start.10
  11.7 4.2 copy-start.16
  11.8 4.9 %copy-start.12 = (bf16[4,256]{1,0:T(4,128)(2,1)S(1)}, bf16[4,256]{1,0:T(4,128)(2,1)}, u32[]{:S(2)}) copy-start(bf16[4,256]{1,0:T(4,128)(2,1)} %param.29) | copy-start | bytes 6148
  11.8 5.5 %copy-start.13 = (bf16[768]{0:T(1024)(128)(2,1)S(1)}, bf16[768]{0:T(1024)(128)(2,1)}, u32[]{:S(2)}) copy-start(bf16[768]{0:T(1024)(128)(2,1)} %param.33) | copy-start | bytes 4612
  12.2 5.7 %copy-start.23 = (u32[128]{0:T(128)S(1)}, u32[128]{0:T(128)}, u32[]{:S(2)}) copy-start(u32[128]{0:T(128)} %constant.63) | copy-start | bytes 1540
  12.5 6.7 %collective-permute-start = (bf16[8,1152]{1,0:T(8,128)(2,1)S(1)}, bf16[8,1152]{1,0:T(8,128)(2,1)S(1)}, u32[]{:S(2)}, u32[]{:S(2)}) collective-permute-start(bf16[8,1152]{1,0:T(8,128)(2,1)S(1)} %pad_maximum_fusion.2), channel_id=1, source_target_pairs={{0,4},{4,8},{8,12},{12,16},{16,20},{20,24},{24,28},{28,32},{32,36}... | collective-permute-start | bytes 55304 | tf_op jit(solution)/shard_map/ppermute | solution.py:208
  97.7 14.8 %all-to-all-start = ((f32[32,4,768]{2,1,0:T(4,128)}), f32[32,4,768]{2,1,0:T(4,128)}, u32[]{:S(2)}, u32[]{:S(2)}) async-start(f32[32,4,768]{2,1,0:T(4,128)} %reshape.89), calls=%async_computation | async-start | bytes 786432 | tf_op jit(solution)/shard_map/all_to_all | solution.py:232
  113.9 8.4 %copy-start.9 = (s32[256]{0:T(256)S(1)}, s32[256]{0:T(256)}, u32[]{:S(2)}) copy-start(s32[256]{0:T(256)} %param.22) | copy-start | bytes 3076
  115.2 16.3 %copy-start.6 = (bf16[256,1536]{1,0:T(8,128)(2,1)S(1)}, bf16[256,1536]{1,0:T(8,128)(2,1)}, u32[]{:S(2)}) copy-start(bf16[256,1536]{1,0:T(8,128)(2,1)} %param.21) | copy-start | bytes 2359300
  118.3 12.0 %all-to-all-start.1 = ((bf16[32,4,768]{2,1,0:T(4,128)(2,1)}), bf16[32,4,768]{2,1,0:T(4,128)(2,1)S(1)}, u32[]{:S(2)}, u32[]{:S(2)}) async-start(bf16[32,4,768]{2,1,0:T(4,128)(2,1)} %reshape.104), calls=%async_computation.1 | async-start | bytes 393216 | tf_op jit(solution)/shard_map/all_to_all | solution.py:236
  122.2 39.6 %reduce-scatter.4.cloned.1.call-start = ((), (), s32[]{:S(2)}) async-start(), calls=%async_computation.5 | async-start | bytes 1966080 | tf_op jit(solution)/shard_map/reduce_scatter | solution.py:246
  136.7 1.4 copy-start.11
  136.7 1.4 copy-start.22
  136.7 76.5 %all-gather.8.cloned.1.call-start = ((), (), s32[]{:S(2)}) async-start(), calls=%async_computation.6 | async-start | bytes 6488064 | tf_op jit(solution)/shard_map/all_gather | solution.py:251
  163.1 0.8 copy-start.3
  163.9 2.2 copy-start.14
  164.7 48.5 %copy-start.18 = (bf16[1536,64]{0,1:T(8,128)(2,1)S(1)}, bf16[1536,64]{0,1:T(8,128)(2,1)}, u32[]{:S(2)}) copy-start(bf16[1536,64]{0,1:T(8,128)(2,1)} %param.36) | copy-start | bytes 589828
  164.7 88.7 %all-gather.12.cloned.1.call-start = ((), (), s32[]{:S(2)}) async-start(), calls=%async_computation.10 | async-start | bytes 3932160 | tf_op jit(solution)/shard_map/all_gather | solution.py:194
  165.5 155.4 %all-gather.10.cloned.1.call-start = ((), (), s32[]{:S(2)}) async-start(), calls=%async_computation.9 | async-start | bytes 7864320 | tf_op jit(solution)/shard_map/all_gather | solution.py:193
  166.0 272.2 %reduce-scatter.6.cloned.1.call-start = ((), (), s32[]{:S(2)}) async-start(), calls=%async_computation.7 | async-start | bytes 6488064 | tf_op jit(solution)/shard_map/reduce_scatter | solution.py:260
  320.9 1.9 copy-start.2
  348.8 2.7 copy-start.1
  351.5 0.9 copy-start.7
  351.5 114.2 %reduce-scatter.8.cloned.1.call-start = ((), (), s32[]{:S(2)}) async-start(), calls=%async_computation.8 | async-start | bytes 1966080 | tf_op jit(solution)/shard_map/reduce_scatter | solution.py:269
  368.6 69.6 %copy-start.4 = (f32[64,1536]{1,0:T(8,128)S(1)}, f32[64,1536]{1,0:T(8,128)}, u32[]{:S(2)}) copy-start(f32[64,1536]{1,0:T(8,128)} %copy-done.3) | copy-start | bytes 1179652
  (1 other events, 0.7 us)
Sparse Core Ops, SparseCore 0:
  136.8 24.9 reduce-scatter.3
  164.8 48.3 all-gather.7
  214.9 38.5 all-gather.11
  255.0 65.8 all-gather.9
  351.7 86.5 reduce-scatter.5
  440.5 25.1 reduce-scatter.7

commit v2 on v1

v2 whole, which is shorter than its diff:
```python
import functools

import jax
import jax.numpy as jnp
from jax import lax
from jax.experimental import pallas as pl
from jax.experimental.pallas import tpu as pltpu
from jax.sharding import PartitionSpec as P

D = 1536
HEAD = 64
NSTATE = 128
DI = 3072
epsilon = 1e-05
highest = lax.Precision.HIGHEST
F32 = jnp.float32
BF = jnp.bfloat16


def rms_apply(values, gain):
    mean_square = jnp.mean(values * values, axis=-1, keepdims=True)
    return values * lax.rsqrt(mean_square + epsilon) * gain.astype(F32)


def silu(v):
    return v / (1.0 + jnp.exp(-v))


MESH = pl.DeviceIdType.MESH


def mixer_kernel(
    heads, seqs, tps, x_ref, bc_ref, idc_ref, idr_ref, dt_ref, rate_ref, cx_ref, cb_ref, skip_ref,
    z_ref, gain_ref, out_ref, tok_ref, moe_gain_ref, resid_ref, moe_ref,
    xs, bs, ids, tail, head_rows, ysum, slabs, got, back, entry, proj, sent, landed, sq_out, sq_in,
    tail_sems, go_sems, come_sems, ret_go, ret_come, tp_go, tp_come, sq_go, sq_come,
):
    me, mt = lax.axis_index("seq"), lax.axis_index("tp")
    n, width = x_ref.shape
    part = n // tps
    half_w = width // 2
    barrier = pltpu.get_barrier_semaphore()

    def greet(d, c):
        pl.semaphore_signal(
            barrier, inc=1, device_id={"seq": lax.rem(me + d, seqs)}, device_id_type=MESH
        )
        return c

    lax.fori_loop(1, seqs, greet, 0)
    for d in range(1, tps):
        pl.semaphore_signal(
            barrier, inc=1, device_id={"tp": lax.rem(mt + d, tps)}, device_id_type=MESH
        )
    xs[pl.ds(8, n), :] = x_ref[...].astype(F32)
    bs[pl.ds(8, n), :] = bc_ref[...].astype(F32)
    own = idc_ref[...]
    ids[pl.ds(8, n), :] = jnp.broadcast_to(own, (n, 128))
    tail[:, 0:width] = xs[pl.ds(n, 8), :]
    tail[:, width : width + 2 * NSTATE] = bs[pl.ds(n, 8), :]
    tail[:, width + 2 * NSTATE :] = ids[pl.ds(n, 8), :]
    pl.semaphore_wait(barrier, seqs - 1 + tps - 1)
    halo = pltpu.make_async_remote_copy(
        src_ref=tail, dst_ref=head_rows, send_sem=tail_sems.at[0], recv_sem=tail_sems.at[1],
        device_id={"seq": lax.rem(me + 1, seqs)}, device_id_type=MESH,
    )
    halo.start()

    raw = dt_ref[...]
    step = jnp.maximum(raw, 0.0) + jnp.log1p(jnp.exp(-jnp.abs(raw)))
    decay = -rate_ref[...] * step
    row = lax.broadcasted_iota(jnp.int32, (n, n), 0)
    col = lax.broadcasted_iota(jnp.int32, (n, n), 1)
    causal = row >= col
    tri = jnp.where(causal, 1.0, 0.0)
    cum = jnp.dot(tri, decay, precision=highest, preferred_element_type=F32)
    cum_t = cum.T
    last = cum[n - 1 : n, :]
    expand = jnp.where(
        lax.broadcasted_iota(jnp.int32, (128, width), 1) // HEAD
        == lax.broadcasted_iota(jnp.int32, (128, width), 0),
        1.0,
        0.0,
    )
    step_w = jnp.dot(step, expand, precision=highest, preferred_element_type=F32)
    at_end = own == idc_ref[n - 1 : n, :]
    to_end = jnp.where(at_end, jnp.exp(last - cum), 0.0)
    end_w = jnp.dot(to_end, expand, precision=highest, preferred_element_type=F32)
    carry_w = jnp.dot(jnp.exp(cum), expand, precision=highest, preferred_element_type=F32)
    r8 = lax.broadcasted_iota(jnp.int32, (NSTATE, 2 * NSTATE), 1)
    n8 = lax.broadcasted_iota(jnp.int32, (NSTATE, 2 * NSTATE), 0)
    same = n8 == 4 * (r8 // 8) + r8 % 4
    dup_l = jnp.where(same & (r8 % 8 < 4), 1.0, 0.0).astype(BF)
    dup_r = jnp.where(same & (r8 % 8 >= 4), 1.0, 0.0).astype(BF)
    dup = dup_l + dup_r
    low = lax.broadcasted_iota(jnp.int32, (2 * NSTATE, half_w), 0) % 8 < 4

    halo.wait()
    xs[pl.ds(0, 8), :] = head_rows[:, 0:width]
    bs[pl.ds(0, 8), :] = head_rows[:, width : width + 2 * NSTATE]
    ids[pl.ds(0, 8), :] = jnp.where(me == 0, -1.0, head_rows[:, width + 2 * NSTATE :])
    before_id = ids[pl.ds(7, 1), :]
    xsum = jnp.zeros((n, width), F32)
    bsum = jnp.zeros((n, 2 * NSTATE), F32)
    for k in range(4):
        live = ids[pl.ds(5 + k, n), 0:1] == own
        xsum += jnp.where(live, xs[pl.ds(5 + k, n), :], 0.0) * cx_ref[k : k + 1, :]
        bsum += jnp.where(live, bs[pl.ds(5 + k, n), :], 0.0) * cb_ref[k : k + 1, :]
    x_conv = silu(xsum).astype(BF).astype(F32)
    bc = silu(bsum).astype(BF)
    b_in, c_out = bc[:, :NSTATE], bc[:, NSTATE:]
    x_step = x_conv * step_w
    x_in = x_step.astype(BF)
    b_dup = jnp.dot(b_in, dup, preferred_element_type=F32).astype(BF)
    state = lax.dot_general(
        b_dup, (x_step * end_w).astype(BF), (((0,), (0,)), ((), ())), preferred_element_type=F32
    )
    state = jnp.where(low, state[:, :half_w], state[:, half_w:])
    slabs[:, :, 0:half_w] = state.reshape(seqs, 8, half_w)
    lane = lax.broadcasted_iota(jnp.int32, (1, 128), 1)
    note = jnp.where(lane == 127, idc_ref[n - 1 : n, :], last)
    slabs[:, :, half_w:] = jnp.broadcast_to(note[None], (seqs, 8, 128))

    def outward(d):
        peer = lax.rem(me + d, seqs)
        return pltpu.make_async_remote_copy(
            src_ref=slabs.at[peer], dst_ref=got.at[me], send_sem=go_sems.at[d],
            recv_sem=come_sems.at[d], device_id={"seq": peer}, device_id_type=MESH,
        )

    def homeward(d):
        peer = lax.rem(me + d, seqs)
        return pltpu.make_async_remote_copy(
            src_ref=back.at[peer], dst_ref=entry.at[me], send_sem=ret_go.at[d],
            recv_sem=ret_come.at[d], device_id={"seq": peer}, device_id_type=MESH,
        )

    def each(make, act):
        def one(d, c):
            getattr(make(d), act)()
            return c

        lax.fori_loop(1, seqs, one, 0)

    each(outward, "start")
    got[me] = slabs[me]

    scores = lax.dot_general(c_out, b_in, (((1,), (1,)), ((), ())), preferred_element_type=F32)
    scores = jnp.where(causal & (own == idr_ref[...]), scores, 0.0)

    def inner(pairs):
        half = n // 2
        for top, bottom in ((0, half), (half, n)):
            for pair in pairs:
                parts = []
                for h in (2 * pair, 2 * pair + 1):
                    diff = cum[top:bottom, h : h + 1] - cum_t[h : h + 1, :bottom]
                    mixing = scores[top:bottom, :bottom] * jnp.exp(jnp.minimum(diff, 0.0))
                    parts.append(
                        jnp.dot(
                            mixing.astype(BF), x_in[:bottom, h * HEAD : (h + 1) * HEAD],
                            preferred_element_type=F32,
                        )
                    )
                cols = slice(pair * 128, pair * 128 + 128)
                ysum[top:bottom, cols] = (
                    jnp.concatenate(parts, axis=1)
                    + x_conv[top:bottom, cols] * skip_ref[:, cols]
                )

    inner(range(0, heads // 4))
    each(outward, "wait")
    notes = got[:, :, half_w:].reshape(8 * seqs, 128)
    faded = jnp.dot(
        jnp.where(lax.broadcasted_iota(jnp.int32, notes.shape, 1) < heads, notes, 0.0),
        expand, precision=highest, preferred_element_type=F32,
    )
    faded = jnp.exp(jnp.where(low, faded[:, :half_w], faded[:, half_w:])).reshape(seqs, 8, half_w)
    ends = jnp.broadcast_to(notes[:, 127:128], (8 * seqs, half_w)).reshape(seqs, 8, half_w)
    running = jnp.zeros((8, half_w), F32)
    for q in range(seqs):
        back[q] = running
        if q == 0:
            running = got[q, :, 0:half_w]
        else:
            keep = jnp.where(ends[q] == ends[q - 1], faded[q], 0.0)
            running = running * keep + got[q, :, 0:half_w]
    each(homeward, "start")
    entry[me] = back[me]
    inner(range(heads // 4, heads // 2))
    c_l = jnp.dot(c_out, dup_l, preferred_element_type=F32).astype(BF)
    c_r = jnp.dot(c_out, dup_r, preferred_element_type=F32).astype(BF)
    zg = z_ref[...].astype(F32)
    gate = silu(zg)
    follows = own == before_id[:, 0:1]
    each(homeward, "wait")
    inc = entry[...].reshape(8 * seqs, half_w).astype(BF)
    before = jnp.concatenate(
        [
            jnp.dot(c_l, inc, preferred_element_type=F32),
            jnp.dot(c_r, inc, preferred_element_type=F32),
        ],
        axis=1,
    )
    scanned = ysum[...] + jnp.where(follows, before * carry_w, 0.0)
    gated = scanned * gate
    squares = jnp.sum(gated * gated, axis=1, keepdims=True)
    sq_out[...] = jnp.broadcast_to(squares, (n, 128)).reshape(tps, part, 128)
    lhs = (gated * gain_ref[...]).astype(BF)
    chunk = 512
    for c in range(D // chunk):
        cols = slice(c * chunk, (c + 1) * chunk)
        piece = jnp.dot(lhs, out_ref[:, cols], preferred_element_type=F32)
        piece = piece.reshape(tps, part, chunk)
        proj[:, :, cols] = piece
        sent[:, :, cols] = piece.astype(BF)
    moves = []
    for d in (2, 1, 3):
        peer = lax.rem(mt + d, tps)
        for src, dst, go, come in (
            (sent, landed, tp_go, tp_come),
            (sq_out, sq_in, sq_go, sq_come),
        ):
            move = pltpu.make_async_remote_copy(
                src_ref=src.at[peer], dst_ref=dst.at[d - 1], send_sem=go.at[d - 1],
                recv_sem=come.at[d - 1], device_id={"tp": peer}, device_id_type=MESH,
            )
            move.start()
            moves.append(move)
    total = proj[mt]
    sq = sq_out[mt]
    for move in moves:
        move.wait()
    for d in range(tps - 1):
        total = total + landed[d].astype(F32)
        sq = sq + sq_in[d]
    resid = tok_ref[...].astype(F32) + total * lax.rsqrt(sq[:, 0:1] / DI + epsilon)
    resid_ref[...] = resid
    power = jnp.sum(resid * resid, axis=1, keepdims=True) / D
    moe_ref[...] = (resid * lax.rsqrt(power + epsilon) * moe_gain_ref[...]).astype(BF)


def mixer(seqs, tps, heads, *args):
    n, width = args[0].shape
    part = n // tps
    vm = pl.BlockSpec(memory_space=pltpu.VMEM)
    dma = pltpu.SemaphoreType.DMA
    return pl.pallas_call(
        functools.partial(mixer_kernel, heads, seqs, tps),
        out_shape=(jax.ShapeDtypeStruct((part, D), F32), jax.ShapeDtypeStruct((part, D), BF)),
        in_specs=[vm] * len(args),
        out_specs=(vm, vm),
        scratch_shapes=[
            pltpu.VMEM((n + 8, width), F32),
            pltpu.VMEM((n + 8, 2 * NSTATE), F32),
            pltpu.VMEM((n + 8, 128), F32),
            pltpu.VMEM((8, width + 2 * NSTATE + 128), F32),
            pltpu.VMEM((8, width + 2 * NSTATE + 128), F32),
            pltpu.VMEM((n, width), F32),
            pltpu.VMEM((seqs, 8, width // 2 + 128), F32),
            pltpu.VMEM((seqs, 8, width // 2 + 128), F32),
            pltpu.VMEM((seqs, 8, width // 2), F32),
            pltpu.VMEM((seqs, 8, width // 2), F32),
            pltpu.VMEM((tps, part, D), F32),
            pltpu.VMEM((tps, part, D), BF),
            pltpu.VMEM((tps - 1, part, D), BF),
            pltpu.VMEM((tps, part, 128), F32),
            pltpu.VMEM((tps - 1, part, 128), F32),
            dma((2,)),
            dma((seqs,)),
            dma((seqs,)),
            dma((seqs,)),
            dma((seqs,)),
            dma((tps - 1,)),
            dma((tps - 1,)),
            dma((tps - 1,)),
            dma((tps - 1,)),
        ],
        compiler_params=pltpu.CompilerParams(collective_id=0, has_side_effects=True),
        name="mixer",
    )(*args)


def expert_kernel(parts, x_ref, w_ref, *rest):
    gus, dns = rest[:parts], rest[parts : 2 * parts]
    o_ref, gu, dn, sem = rest[2 * parts :]
    experts, wide = gus[0].shape[0], gus[0].shape[3]

    def copies():
        out = []
        for t in range(parts):
            for e in range(experts):
                for c in range(2):
                    out.append(
                        pltpu.make_async_copy(
                            gus[t].at[e, c],
                            gu.at[e, :, pl.ds((c * parts + t) * wide, wide)],
                            sem.at[len(out)],
                        )
                    )
                out.append(
                    pltpu.make_async_copy(
                        dns[t].at[e], dn.at[e, pl.ds(t * wide, wide), :], sem.at[len(out)]
                    )
                )
        return out

    @pl.when(pl.program_id(0) == 0)
    def _():
        for copy in copies():
            copy.start()
        for copy in copies():
            copy.wait()

    x = x_ref[...]
    total = None
    hidden = parts * wide
    for e in range(experts):
        both = jnp.dot(x, gu[e], preferred_element_type=F32)
        act = (silu(both[:, :hidden]) * both[:, hidden:] * w_ref[:, e : e + 1]).astype(BF)
        out = jnp.dot(act, dn[e], preferred_element_type=F32)
        total = out if total is None else total + out
    o_ref[...] = total.astype(BF)


def experts_dense(x, wts, gate_up, down):
    rows = x.shape[0]
    parts = len(gate_up)
    experts, _, _, wide = gate_up[0].shape
    tile = 256
    hidden = parts * wide
    return pl.pallas_call(
        functools.partial(expert_kernel, parts),
        out_shape=jax.ShapeDtypeStruct((rows, D), BF),
        grid=(rows // tile,),
        in_specs=[
            pl.BlockSpec((tile, D), lambda i: (i, 0)),
            pl.BlockSpec((tile, experts), lambda i: (i, 0)),
        ]
        + [pl.BlockSpec(memory_space=pl.ANY)] * (2 * parts),
        out_specs=pl.BlockSpec((tile, D), lambda i: (i, 0)),
        scratch_shapes=[
            pltpu.VMEM((experts, D, 2 * hidden), BF),
            pltpu.VMEM((experts, hidden, D), BF),
            pltpu.SemaphoreType.DMA((parts * experts * 3,)),
        ],
        compiler_params=pltpu.CompilerParams(vmem_limit_bytes=40 << 20),
        name="experts_dense",
    )(x, wts, *gate_up, *down)


def body(
    tokens, doc_ids, mix_gain, zgate_proj, xin_proj, bc_proj, dt_proj, conv_x, conv_bc, dt_bias,
    decay_rate, skip_gain, norm_gain, out_proj, moe_gain, router, routes, expert_gate_up,
    expert_down, shared_gate_up, shared_down,
):
    rows = tokens.shape[0]
    tp_index, seq_index = lax.axis_index("tp"), lax.axis_index("seq")
    tp_count, seq_count = lax.axis_size("tp"), lax.axis_size("seq")
    heads = dt_proj.shape[1]
    width = heads * HEAD
    part = rows // tp_count
    experts_local = expert_down.shape[0]

    def shift(value, steps):
        pairs = [(t, (t + steps) % tp_count) for t in range(tp_count)]
        return lax.ppermute(value, "tp", pairs)

    gu_left, dn_left = shift(expert_gate_up, 1), shift(expert_down, 1)
    gu_right, dn_right = shift(expert_gate_up, -1), shift(expert_down, -1)
    own_routes = lax.dynamic_slice_in_dim(routes, tp_index * part, part, 0)
    plane_routes = lax.all_gather(own_routes, "seq", tiled=True)

    resid_in = tokens.astype(F32)
    normed_in = rms_apply(resid_in, mix_gain).astype(BF)
    zgate = jnp.dot(normed_in, zgate_proj, preferred_element_type=F32).astype(BF)
    x_pre = jnp.dot(normed_in, xin_proj, preferred_element_type=F32).astype(BF)
    bc_pre = jnp.dot(normed_in, bc_proj, preferred_element_type=F32).astype(BF)
    dt_raw = jnp.dot(normed_in, dt_proj, preferred_element_type=F32) + dt_bias
    dt_raw = jnp.pad(dt_raw, ((0, 0), (0, 128 - heads)))
    rate = jnp.pad(decay_rate, (0, 128 - heads))[None, :]
    own_rows = lax.dynamic_slice_in_dim(tokens, tp_index * part, part, 0)
    ids = doc_ids.astype(F32)
    resid, moe_in = mixer(
        seq_count, tp_count, heads, x_pre, bc_pre, ids[:, None], ids[None, :], dt_raw, rate,
        conv_x.astype(F32), conv_bc.astype(F32), jnp.repeat(skip_gain, HEAD)[None, :], zgate,
        norm_gain.astype(F32)[None, :], out_proj, own_rows, moe_gain.astype(F32)[None, :],
    )
    moe_in, resid, gu_left, dn_right = lax.optimization_barrier(
        (moe_in, resid, gu_left, dn_right)
    )
    gu_far, dn_far = shift(gu_left, 1), shift(dn_right, -1)

    plane = lax.all_gather(moe_in, "seq", tiled=True)
    line = lax.all_gather(moe_in, "tp", tiled=True)
    logits = jnp.dot(plane, router, preferred_element_type=F32)
    iota = jnp.arange(router.shape[1], dtype=jnp.int32)
    named = jnp.any(plane_routes[:, :, None] == iota[None, None, :], axis=1)
    sigmas = jnp.where(named, jax.nn.sigmoid(logits), 0.0)
    wts = sigmas / jnp.sum(sigmas, axis=1, keepdims=True)
    wts = lax.dynamic_slice_in_dim(wts, seq_index * experts_local, experts_local, 1)
    routed = experts_dense(
        plane, wts, (expert_gate_up, gu_left, gu_right, gu_far),
        (expert_down, dn_left, dn_right, dn_far),
    )
    routed = lax.psum_scatter(routed, "seq", scatter_dimension=0, tiled=True)
    shared_gate = jnp.dot(line, shared_gate_up[0], preferred_element_type=F32)
    shared_up = jnp.dot(line, shared_gate_up[1], preferred_element_type=F32)
    shared_act = (jax.nn.silu(shared_gate) * shared_up).astype(BF)
    shared_part = jnp.dot(shared_act, shared_down, preferred_element_type=F32)
    mine = lax.dynamic_slice_in_dim(shared_part, tp_index * part, part, 0)
    whole = lax.dynamic_update_slice_in_dim(
        shared_part, mine + resid + routed.astype(F32), tp_index * part, 0
    )
    added = lax.psum_scatter(whole, "tp", scatter_dimension=1, tiled=True)
    return added.astype(BF)


def solution(mesh):
    in_specs = (
        P("seq", None), P("seq"), P(), P(None, "tp"), P(None, "tp"), P(), P(None, "tp"),
        P(None, "tp"), P(), P("tp"), P("tp"), P("tp"), P("tp"), P("tp", None), P(), P(),
        P("seq", None), P("seq", None, None, "tp"), P("seq", "tp", None), P(None, None, "tp"),
        P("tp", None),
    )
    return jax.shard_map(
        body, mesh=mesh, in_specs=in_specs, out_specs=P("seq", "tp"), check_vma=False
    )
```

time: 475 us -> 271 us (0.57)
  waiting for transfers between devices: 243 us -> 107 us
  blocking collectives: 118 us -> 38 us
  Pallas kernels: 31.3 us -> 71.6 us
  local copies, waits for them, and re-layouts: 19.1 us -> 6.1 us
  other arithmetic: 16 us -> 7.93 us
  matrix products: 21.9 us -> 16.6 us
    all_gather x2 -> x0, waiting for transfers between devices: 102 us -> none  [the longest x1 67.4 us: body(): gate_up_all = lax.all_gather(expert_gate_up, 'tp')]
    unnamed x2 -> x0, blocking collectives: 79.5 us -> none
    pallas_call x2, Pallas kernels: 31.3 us -> 71.6 us  [the longest x1 43.6 us: mixer(): pl.pallas_call(functools.partial(mixer_kernel, heads, seqs, tps), out_sha...]
    all_to_all x2 -> x0, waiting for transfers between devices: 15.8 us -> none  [body(): lax.all_to_all(share, 'seq', split_axis=0, concat_axis=0, tiled=True)]
    reduce_scatter x1 -> x0, waiting for transfers between devices: 10.3 us -> none  [body(): lax.psum_scatter(projected, 'tp', scatter_dimension=0, tiled=True)]
    ppermute x1 -> x6, starting transfers between devices: 1.28 us -> 9.95 us  [shift(): return lax.ppermute(value, 'tp', pairs)]
    all_to_all x2 -> x0, starting transfers between devices: 8.46 us -> none  [body(): lax.all_to_all(share, 'seq', split_axis=0, concat_axis=0, tiled=True)]
    unnamed x54 -> x36, local copies, waits for them, and re-layouts: 7.78 us -> 1.14 us
  transfers between devices with their start and end apart: 9 -> 9, of which waited for: 8 -> 4; matrix products, arithmetic and copies ran while one was open for 5% -> 10% of each run, Pallas kernels for 0% -> 16%
where the time goes in v2:
time: 271 us
  waiting for transfers between devices  107 us (39%)
  Pallas kernels  71.6 us (26%)
  blocking collectives  38 us (14%)
  matrix products  16.6 us (6%)
  between operations  13.3 us (5%)
  starting transfers between devices  10 us (4%)
  other arithmetic  7.93 us (3%)
  local copies, waits for them, and re-layouts  6.1 us (2%)
    reduce_scatter x1, waiting for transfers between devices, body(): routed = lax.psum_scatter(routed, 'seq', scatter_dimension=0, tiled=True)  62.3 us
    pallas_call x1, Pallas kernels, mixer(): pl.pallas_call(functools.partial(mixer_kernel, heads, seqs, tps), out_sha...  43.6 us
    pallas_call x1, Pallas kernels, experts_dense(): pl.pallas_call(functools.partial(expert_kernel, parts), out_shape=jax.Sha...  28 us
    reduce_scatter x1, waiting for transfers between devices, body(): added = lax.psum_scatter(whole, 'tp', scatter_dimension=1, tiled=True)  25.8 us
    all_gather x1, blocking collectives, body(): plane_routes = lax.all_gather(own_routes, 'seq', tiled=True)  23.9 us
    all_gather x1, waiting for transfers between devices, body(): plane = lax.all_gather(moe_in, 'seq', tiled=True)  16.5 us
    all_gather x1, blocking collectives, body(): line = lax.all_gather(moe_in, 'tp', tiled=True)  14.1 us
    ppermute x6, starting transfers between devices, shift(): return lax.ppermute(value, 'tp', pairs)  9.95 us
  transfers between devices with their start and end apart: 9, of which 4 were waited for; matrix products, arithmetic and copies ran while one was open for 10% of the time, Pallas kernels for 16%

profile of v2, /device:TPU:0, one launch (start us, length us, event | category | flops | bytes accessed | tf_op | source)
XLA Modules:
  0.0 271.0 jit_solution(947701308601986822)
XLA Ops:
  6.5 2.0 collective-permute-start
  8.6 2.2 collective-permute-start.1
  10.8 1.4 fusion.5
  12.2 0.7 convert_element_type.43
  12.8 1.7 convolution_add_fusion
  14.6 1.1 convolution_convert_fusion.2.bc_ref
  15.7 0.7 constant_dynamic-slice_fusion.tok_ref
  16.4 0.8 copy.40.idc_ref
  17.2 0.6 convert_element_type.48.cx_ref
  17.9 0.7 broadcast_in_dim_reshape.3.skip_ref
  18.5 0.6 reshape.13.moe_gain_ref
  20.3 0.7 pad.8.dt_ref
  21.5 1.6 convolution_convert_fusion.z_ref
  23.2 1.6 convolution_convert_fusion.1.x_ref
  24.8 43.6 %mixer.1 = (f32[64,1536]{1,0:T(8,128)}, bf16[64,1536]{1,0:T(8,128)(2,1)}) custom-call(bf16[256,768]{1,0:T(8,128)(2,1)} %convolution_convert_fusion.1.x_ref, bf16[256,256]{1,0:T(8,128)(2,1)} %convolution_convert_fusion.2.bc_ref, f32[256,1]{1,0:T(8,128)} %copy.40.idc_ref, f32[1,256]{1,0:T(1,128)} %bitcast.25, f32[256,128]{1,0:T(8,128)} %pad.8.dt_ref, ...), custom_call_target="tpu_custom_call" | custom-call | tf_op jit(solution)/shard_map/mixer/pallas_call | solution.py:248
  68.4 0.8 collective-permute-start.2
  69.2 1.3 collective-permute-start.3
  71.1 23.9 %all-gather = s32[32,64,6]{1,2,0:T(8,128)S(1)} all-gather(s32[1,64,6]{1,2,0:T(8,128)S(1)} %dynamic-slice_bitcast_fusion), channel_id=1, replica_groups=mesh['seq'=32,'tp'=4] {'seq'}, dimensions={0}, use_global_device_ids=true | all-gather | bytes 50688 | tf_op jit(solution)/shard_map/all_gather | solution.py:372
  95.9 3.2 %collective-permute-start.5 = (bf16[2,128,1536]{2,1,0:T(8,128)(2,1)}, bf16[2,128,1536]{2,1,0:T(8,128)(2,1)}, u32[]{:S(2)}, u32[]{:S(2)}) collective-permute-start(bf16[2,128,1536]{2,1,0:T(8,128)(2,1)} %collective-permute-done.1.rest_6_), channel_id=1, source_target_pairs={{0,3},{1,0},{2,1},{3,2},{4,7},{5,4},{6,5},{7,6},{8,11},{9,8},{10,9... | collective-permute-start | bytes 2359304 | tf_op jit(solution)/shard_map/ppermute | solution.py:367
  99.1 16.5 %all-gather.3.cloned.1.call-done.x_ref = bf16[2048,1536]{1,0:T(8,128)(2,1)} async-done(((bf16[64,1536]{1,0:T(8,128)(2,1)}), bf16[2048,1536]{1,0:T(8,128)(2,1)}) %all-gather.3.cloned.1.call-update) | async-done | bytes 6291472 | tf_op jit(solution)/shard_map/all_gather | solution.py:394
  115.6 4.7 %fusion.28 = (f32[2048]{0:T(1024)S(1)}, f32[2048,64]{1,0:T(8,128)S(1)}) fusion(pred[2048,64]{1,0:T(32,128)(4,1)S(1)} %copy.43, bf16[2048,1536]{1,0:T(8,128)(2,1)} %all-gather.3.cloned.1.call-done.x_ref, bf16[1536,64]{0,1:T(8,128)(2,1)} %param.36), kind=kOutput, calls=%fused_computation.37 | convolution fusion | flops 403306496 | bytes 7151616 | tf_op jit(solution)/shard_map/dot_general | solution.py:396
  120.3 0.6 dynamic-slice_divide_fusion.w_ref
  120.9 2.7 %collective-permute-done.4.rest_5_ = bf16[2,128,1536]{2,1,0:T(8,128)(2,1)} collective-permute-done((bf16[2,128,1536]{2,1,0:T(8,128)(2,1)S(1)}, bf16[2,128,1536]{2,1,0:T(8,128)(2,1)}, u32[]{:S(2)}, u32[]{:S(2)}) %collective-permute-start.4) | collective-permute-done | bytes 786464 | tf_op jit(solution)/shard_map/ppermute | solution.py:367
  123.7 28.0 %experts_dense.1 = bf16[2048,1536]{1,0:T(8,128)(2,1)} custom-call(bf16[2048,1536]{1,0:T(8,128)(2,1)} %all-gather.3.cloned.1.call-done.x_ref, f32[2048,2]{1,0:T(8,128)S(1)} %dynamic-slice_divide_fusion.w_ref, bf16[2,2,1536,128]{3,2,1,0:T(8,128)(2,1)S(1)} %copy-done.1, bf16[2,2,1536,128]{3,2,1,0:T(8,128)(2,1)} %collective-permute-done.rest_1_, ...), custom_call_target="tpu_custom_call" | custom-call | tf_op jit(solution)/shard_map/experts_dense/pallas_call | solution.py:332
  151.8 0.8 copy-done.4
  152.6 14.1 %all_gather.9 = bf16[256,1536]{1,0:T(8,128)(2,1)S(1)} all-gather(bf16[64,1536]{1,0:T(8,128)(2,1)S(1)} %copy-done.4), channel_id=1, replica_groups=mesh['seq'=32,'tp'=4] {'tp'}, dimensions={0}, use_global_device_ids=true | all-gather | bytes 983040 | tf_op jit(solution)/shard_map/all_gather | solution.py:395
  166.7 2.3 fusion.12
  169.0 3.8 %fusion.9 = f32[256,1536]{1,0:T(8,128)} fusion(bf16[256,1536]{1,0:T(8,128)(2,1)} %param.41, bf16[256,1536]{1,0:T(8,128)(2,1)S(1)} %all_gather.9, bf16[2,1536,256]{2,1,0:T(8,128)(2,1)} %param.40, f32[256,256]{1,0:T(8,128)} %fusion.12), kind=kOutput, calls=%fused_computation.18 | convolution fusion | flops 403046400 | bytes 4194304 | tf_op jit(solution)/shard_map/dot_general | solution.py:410
  172.7 62.3 %reduce-scatter.3.cloned.1.call-done = bf16[64,1536]{1,0:T(8,128)(2,1)} async-done(((bf16[2048,1536]{1,0:T(8,128)(2,1)}), bf16[64,1536]{1,0:T(8,128)(2,1)}) %reduce-scatter.3.cloned.1.call-update) | async-done | bytes 196624 | tf_op jit(solution)/shard_map/reduce_scatter | solution.py:406
  235.1 1.9 add_dynamic-update-slice_fusion
  237.0 25.8 %reduce-scatter.5.cloned.1.call-done = f32[256,384]{1,0:T(8,128)} async-done(((f32[256,1536]{1,0:T(8,128)}), f32[256,384]{1,0:T(8,128)}) %reduce-scatter.5.cloned.1.call-update) | async-done | bytes 393232 | tf_op jit(solution)/shard_map/reduce_scatter | solution.py:415
  262.8 1.7 convert_element_type.53
  (56 shorter events, 3.6 us)
Async XLA Ops:
  6.5 15.0 %copy-start = (bf16[1536,768]{1,0:T(8,128)(2,1)S(1)}, bf16[1536,768]{1,0:T(8,128)(2,1)}, u32[]{:S(2)}) copy-start(bf16[1536,768]{1,0:T(8,128)(2,1)} %param.24) | copy-start | bytes 7077892
  6.5 8.0 %copy-start.3 = (bf16[256,1536]{1,0:T(8,128)(2,1)S(1)}, bf16[256,1536]{1,0:T(8,128)(2,1)}, u32[]{:S(2)}) copy-start(bf16[256,1536]{1,0:T(8,128)(2,1)} %param.21) | copy-start | bytes 2359300
  6.5 109.1 %all-gather.3.cloned.1.call-start = ((), (), s32[]{:S(2)}) async-start(), calls=%async_computation.2 | async-start | bytes 6488064 | tf_op jit(solution)/shard_map/all_gather | solution.py:394
  6.5 61.8 %collective-permute-start = (bf16[2,2,1536,128]{3,2,1,0:T(8,128)(2,1)}, bf16[2,2,1536,128]{3,2,1,0:T(8,128)(2,1)}, u32[]{:S(2)}, u32[]{:S(2)}) collective-permute-start(bf16[2,2,1536,128]{3,2,1,0:T(8,128)(2,1)} %rest_0_.1), channel_id=1, source_target_pairs={{0,1},{1,2},{2,3},{3,0},{4,5},{5,6},{6,7},{7,4},{8,9},{9,10},{10,1... | collective-permute-start | bytes 4718600 | tf_op jit(solution)/shard_map/ppermute | solution.py:367
  8.6 59.8 %collective-permute-start.1 = (bf16[2,128,1536]{2,1,0:T(8,128)(2,1)}, bf16[2,128,1536]{2,1,0:T(8,128)(2,1)}, u32[]{:S(2)}, u32[]{:S(2)}) collective-permute-start(bf16[2,128,1536]{2,1,0:T(8,128)(2,1)} %rest_4_.1), channel_id=1, source_target_pairs={{0,3},{1,0},{2,1},{3,2},{4,7},{5,4},{6,5},{7,6},{8,11},{9,8},{10,9... | collective-permute-start | bytes 2359304 | tf_op jit(solution)/shard_map/ppermute | solution.py:367
  12.8 1.7 copy-start.15
  14.5 1.9 copy-start.12
  14.5 2.6 copy-start.7
  14.6 3.2 %copy-start.13 = (f32[12]{0:T(128)S(1)}, f32[12]{0:T(128)}, u32[]{:S(2)}) copy-start(f32[12]{0:T(128)} %param.32) | copy-start | bytes 148
  14.6 4.0 %copy-start.8 = (bf16[1536]{0:T(1024)(128)(2,1)S(1)}, bf16[1536]{0:T(1024)(128)(2,1)}, u32[]{:S(2)}) copy-start(bf16[1536]{0:T(1024)(128)(2,1)} %param.35) | copy-start | bytes 9220
  14.6 4.5 %copy-start.9 = (bf16[4,256]{1,0:T(4,128)(2,1)S(1)}, bf16[4,256]{1,0:T(4,128)(2,1)}, u32[]{:S(2)}) copy-start(bf16[4,256]{1,0:T(4,128)(2,1)} %param.29) | copy-start | bytes 6148
  14.6 5.1 %copy-start.11 = (bf16[768]{0:T(1024)(128)(2,1)S(1)}, bf16[768]{0:T(1024)(128)(2,1)}, u32[]{:S(2)}) copy-start(bf16[768]{0:T(1024)(128)(2,1)} %param.33) | copy-start | bytes 4612
  14.6 6.4 %copy-start.16 = (f32[12]{0:T(128)S(1)}, f32[12]{0:T(128)}, u32[]{:S(2)}) copy-start(f32[12]{0:T(128)} %param.31) | copy-start | bytes 148
  16.4 6.7 %copy-start.6 = (f32[256]{0:T(256)}, f32[256]{0:T(256)S(1)}, u32[]{:S(2)}) copy-start(f32[256]{0:T(256)S(1)} %convert_element_type.47) | copy-start | bytes 3076
  21.5 1.7 copy-start.14
  24.8 45.8 %copy-start.2 = (bf16[2,128,1536]{2,1,0:T(8,128)(2,1)S(1)}, bf16[2,128,1536]{2,1,0:T(8,128)(2,1)}, u32[]{:S(2)}) copy-start(bf16[2,128,1536]{2,1,0:T(8,128)(2,1)} %rest_4_.1) | copy-start | bytes 2359300
  24.8 46.3 %copy-start.10 = (s32[256,6]{0,1:T(8,128)S(1)}, s32[256,6]{0,1:T(8,128)}, u32[]{:S(2)}) copy-start(s32[256,6]{0,1:T(8,128)} %param.37) | copy-start | bytes 18436
  68.4 166.7 %reduce-scatter.3.cloned.1.call-start = ((), (), s32[]{:S(2)}) async-start(), calls=%async_computation.3 | async-start | bytes 6488064 | tf_op jit(solution)/shard_map/reduce_scatter | solution.py:406
  68.4 55.2 %collective-permute-start.2 = (bf16[2,2,1536,128]{3,2,1,0:T(8,128)(2,1)}, bf16[2,2,1536,128]{3,2,1,0:T(8,128)(2,1)}, u32[]{:S(2)}, u32[]{:S(2)}) collective-permute-start(bf16[2,2,1536,128]{3,2,1,0:T(8,128)(2,1)} %rest_0_.1), channel_id=1, source_target_pairs={{0,3},{1,0},{2,1},{3,2},{4,7},{5,4},{6,5},{7,6},{8,11},{9,8},{10,9... | collective-permute-start | bytes 4718600 | tf_op jit(solution)/shard_map/ppermute | solution.py:367
  69.2 54.5 %collective-permute-start.3 = (bf16[2,2,1536,128]{3,2,1,0:T(8,128)(2,1)}, bf16[2,2,1536,128]{3,2,1,0:T(8,128)(2,1)}, u32[]{:S(2)}, u32[]{:S(2)}) collective-permute-start(bf16[2,2,1536,128]{3,2,1,0:T(8,128)(2,1)} %collective-permute-done.rest_1_), channel_id=1, source_target_pairs={{0,1},{1,2},{2,3},{3,0},{4,5},{5,6},{6,7},{7,4},{8,9},{9,10},{10,1... | collective-permute-start | bytes 4718600 | tf_op jit(solution)/shard_map/ppermute | solution.py:367
  70.5 53.1 %collective-permute-start.4 = (bf16[2,128,1536]{2,1,0:T(8,128)(2,1)S(1)}, bf16[2,128,1536]{2,1,0:T(8,128)(2,1)}, u32[]{:S(2)}, u32[]{:S(2)}) collective-permute-start(bf16[2,128,1536]{2,1,0:T(8,128)(2,1)S(1)} %copy-done.2), channel_id=1, source_target_pairs={{0,1},{1,2},{2,3},{3,0},{4,5},{5,6},{6,7},{7,4},{8,9},{9,10},{10,1... | collective-permute-start | bytes 2359304 | tf_op jit(solution)/shard_map/ppermute | solution.py:367
  95.9 27.7 %collective-permute-start.5 = (bf16[2,128,1536]{2,1,0:T(8,128)(2,1)}, bf16[2,128,1536]{2,1,0:T(8,128)(2,1)}, u32[]{:S(2)}, u32[]{:S(2)}) collective-permute-start(bf16[2,128,1536]{2,1,0:T(8,128)(2,1)} %collective-permute-done.1.rest_6_), channel_id=1, source_target_pairs={{0,3},{1,0},{2,1},{3,2},{4,7},{5,4},{6,5},{7,6},{8,11},{9,8},{10,9... | collective-permute-start | bytes 2359304 | tf_op jit(solution)/shard_map/ppermute | solution.py:367
  120.3 3.4 %copy-start.1 = (bf16[2,2,1536,128]{3,2,1,0:T(8,128)(2,1)S(1)}, bf16[2,2,1536,128]{3,2,1,0:T(8,128)(2,1)}, u32[]{:S(2)}) copy-start(bf16[2,2,1536,128]{3,2,1,0:T(8,128)(2,1)} %rest_0_.1) | copy-start | bytes 4718596
  151.7 0.9 copy-start.4
  151.7 111.1 %reduce-scatter.5.cloned.1.call-start = ((), (), s32[]{:S(2)}) async-start(), calls=%async_computation.4 | async-start | bytes 1966080 | tf_op jit(solution)/shard_map/reduce_scatter | solution.py:415
  169.0 66.1 %copy-start.5 = (f32[64,1536]{1,0:T(8,128)S(1)}, f32[64,1536]{1,0:T(8,128)}, u32[]{:S(2)}) copy-start(f32[64,1536]{1,0:T(8,128)} %get-tuple-element.14) | copy-start | bytes 1179652
Sparse Core Ops, SparseCore 0:
  68.5 47.0 all-gather.2
  151.9 83.1 reduce-scatter.2
  237.5 25.2 reduce-scatter.4

commit v3 on v2

--- a/solution.py
+++ b/solution.py
@@ -10,6 +10,7 @@
 D = 1536
 HEAD = 64
 NSTATE = 128
+LANES = 128
 DI = 3072
 epsilon = 1e-05
 highest = lax.Precision.HIGHEST
@@ -31,7 +32,7 @@
 
 def mixer_kernel(
     heads, seqs, tps, x_ref, bc_ref, idc_ref, idr_ref, dt_ref, rate_ref, cx_ref, cb_ref, skip_ref,
-    z_ref, gain_ref, out_ref, tok_ref, moe_gain_ref, resid_ref, moe_ref,
+    z_ref, gain_ref, out_ref, tok_ref, moe_gain_ref, router_ref, routes_ref, resid_ref, unit_ref,
     xs, bs, ids, tail, head_rows, ysum, slabs, got, back, entry, proj, sent, landed, sq_out, sq_in,
     tail_sems, go_sems, come_sems, ret_go, ret_come, tp_go, tp_come, sq_go, sq_come,
 ):
@@ -237,7 +238,18 @@
     resid = tok_ref[...].astype(F32) + total * lax.rsqrt(sq[:, 0:1] / DI + epsilon)
     resid_ref[...] = resid
     power = jnp.sum(resid * resid, axis=1, keepdims=True) / D
-    moe_ref[...] = (resid * lax.rsqrt(power + epsilon) * moe_gain_ref[...]).astype(BF)
+    moe_in = (resid * lax.rsqrt(power + epsilon) * moe_gain_ref[...]).astype(BF)
+    unit_ref[:, 0:D] = moe_in
+    logits = jnp.dot(moe_in, router_ref[...], preferred_element_type=F32)
+    expert = lax.broadcasted_iota(jnp.int32, logits.shape, 1)
+    named = expert == routes_ref[:, 0:1]
+    for k in range(1, routes_ref.shape[1]):
+        named = named | (expert == routes_ref[:, k : k + 1])
+    sigmas = jnp.where(named, 1.0 / (1.0 + jnp.exp(-logits)), 0.0)
+    wts = sigmas / jnp.sum(sigmas, axis=1, keepdims=True)
+    unit_ref[:, D:] = jnp.concatenate(
+        [wts, jnp.zeros((part, LANES - wts.shape[1]), F32)], axis=1
+    ).astype(BF)
 
 
 def mixer(seqs, tps, heads, *args):
@@ -247,7 +259,10 @@
     dma = pltpu.SemaphoreType.DMA
     return pl.pallas_call(
         functools.partial(mixer_kernel, heads, seqs, tps),
-        out_shape=(jax.ShapeDtypeStruct((part, D), F32), jax.ShapeDtypeStruct((part, D), BF)),
+        out_shape=(
+            jax.ShapeDtypeStruct((part, D), F32),
+            jax.ShapeDtypeStruct((part, D + LANES), BF),
+        ),
         in_specs=[vm] * len(args),
         out_specs=(vm, vm),
         scratch_shapes=[
@@ -281,72 +296,350 @@
     )(*args)
 
 
-def expert_kernel(parts, x_ref, w_ref, *rest):
-    gus, dns = rest[:parts], rest[parts : 2 * parts]
-    o_ref, gu, dn, sem = rest[2 * parts :]
-    experts, wide = gus[0].shape[0], gus[0].shape[3]
-
-    def copies():
-        out = []
-        for t in range(parts):
-            for e in range(experts):
-                for c in range(2):
-                    out.append(
-                        pltpu.make_async_copy(
-                            gus[t].at[e, c],
-                            gu.at[e, :, pl.ds((c * parts + t) * wide, wide)],
-                            sem.at[len(out)],
-                        )
-                    )
-                out.append(
-                    pltpu.make_async_copy(
-                        dns[t].at[e], dn.at[e, pl.ds(t * wide, wide), :], sem.at[len(out)]
-                    )
+NX, NY, NC = 4, 4, 2
+
+
+def moe_kernel(
+    tps, unit, resid, gu_own, gu_left, gu_right, dn_own, dn_left, dn_right, sgu, sdn, out,
+    plane, line, gu, dn, away, partner, sums, b_in, a_in, b2_in, a2_in, sh_out, sh_in, fin_out,
+    fin_in, acc, send, recv, tp_send, tp_recv, far_send, far_recv, load_sem, core_send, core_recv,
+):
+    me, mt = lax.axis_index("seq"), lax.axis_index("tp")
+    c, x, y = lax.rem(me, NC), lax.rem(me // NC, NX), me // (NC * NX)
+    rows = unit.shape[0]
+    experts, wide = gu_own.shape[0], gu_own.shape[3]
+    half, quarter = rows // 2, rows // 4
+    count = [0]
+
+    def wrap(v, n):
+        return lax.rem(v + n, n)
+
+    def near(d, s):
+        if d == "x":
+            return (y * NX + wrap(x + s, NX)) * NC + c
+        if d == "y":
+            return (wrap(y + s, NY) * NX + x) * NC + c
+        return (y * NX + x) * NC + (1 - c)
+
+    def send_to(src, dst, dev):
+        i = count[0]
+        count[0] += 1
+        move = pltpu.make_async_remote_copy(
+            src_ref=src, dst_ref=dst, send_sem=send.at[i], recv_sem=recv.at[i],
+            device_id={"seq": dev}, device_id_type=MESH,
+        )
+        move.start()
+        return move
+
+    barrier = pltpu.get_barrier_semaphore()
+    for d, s in (("x", 1), ("x", -1), ("y", 1), ("y", -1), ("c", 1)):
+        pl.semaphore_signal(barrier, inc=1, device_id={"seq": near(d, s)}, device_id_type=MESH)
+    for d in range(1, tps):
+        pl.semaphore_signal(
+            barrier, inc=1, device_id={"tp": lax.rem(mt + d, tps)}, device_id_type=MESH
+        )
+    loads = []
+
+    def load(src, dst):
+        copy = pltpu.make_async_copy(src, dst, load_sem.at[len(loads)])
+        copy.start()
+        loads.append(copy)
+
+    def columns(k, slot):
+        return pl.ds((k * tps + slot) * wide, wide)
+
+    for slot, (g, w) in enumerate(((gu_own, dn_own), (gu_left, dn_left), (gu_right, dn_right))):
+        for e in range(experts):
+            for k in range(2):
+                load(g.at[e, k], gu.at[e, :, columns(k, slot)])
+            load(w.at[e], dn.at[e, pl.ds(slot * wide, wide), :])
+    plane[y, x, c] = unit[...]
+    pl.semaphore_wait(barrier, 5 + tps - 1)
+
+    later = []
+
+    def place(d1, o1, d2, o2):
+        off = {d1: o1, d2: o2}
+        return plane.at[wrap(y + off["y"], NY), wrap(x + off["x"], NX), c]
+
+    plans = (("y", "x", 0), ("x", "y", half))
+    own_rows = [unit.at[pl.ds(r0, half)] for _, _, r0 in plans]
+
+    def block(p, o1, o2, start=0, size=half):
+        d1, d2, r0 = plans[p]
+        return place(d1, o1, d2, o2).at[pl.ds(r0 + start, size)]
+
+    def share(p, o1, o2):
+        later.append(
+            send_to(own_rows[p] if (o1, o2) == (0, 0) else block(p, o1, o2), block(p, o1, o2),
+                    near("c", 1))
+        )
+
+    first, second, relay, relay2 = {}, {}, {}, {}
+    for p in (0, 1):
+        d1, d2, _ = plans[p]
+        for s in (1, -1):
+            first[p, s] = send_to(own_rows[p], block(p, 0, 0), near(d1, s))
+    for d in (2, 1, 3):
+        peer = lax.rem(mt + d, tps)
+        move = pltpu.make_async_remote_copy(
+            src_ref=unit, dst_ref=line.at[d - 1], send_sem=tp_send.at[d - 1],
+            recv_sem=tp_recv.at[d - 1], device_id={"tp": peer}, device_id_type=MESH,
+        )
+        move.start()
+        later.append(move)
+    lines = later[-(tps - 1) :]
+    far = []
+    for e, s, g, w in ((0, 1, gu_left, dn_left), (1, tps - 1, gu_right, dn_right)):
+        pieces = [(g.at[e, k], gu.at[e, :, columns(k, tps - 1)]) for k in range(2)]
+        pieces.append((w.at[e], dn.at[e, pl.ds((tps - 1) * wide, wide), :]))
+        for src, dst in pieces:
+            move = pltpu.make_async_remote_copy(
+                src_ref=src, dst_ref=dst, send_sem=far_send.at[len(far)],
+                recv_sem=far_recv.at[len(far)], device_id={"tp": lax.rem(mt + s, tps)},
+                device_id_type=MESH,
+            )
+            move.start()
+            far.append(move)
+    for p in (0, 1):
+        d1, d2, _ = plans[p]
+        for s in (1, -1):
+            second[p, 0, s] = send_to(own_rows[p], block(p, 0, 0), near(d2, s))
+        share(p, 0, 0)
+    for s, start in ((1, 0), (-1, quarter)):
+        for p in (0, 1):
+            d1, d2, _ = plans[p]
+            first[p, s].wait_recv()
+            piece = block(p, -s, 0, start, quarter)
+            relay[p, s] = send_to(piece, piece, near(d1, s))
+            for t in (1, -1):
+                second[p, -s, t] = send_to(block(p, -s, 0), block(p, -s, 0), near(d2, t))
+            share(p, -s, 0)
+    for p in (0, 1):
+        d1, d2, _ = plans[p]
+        relay[p, 1].wait_recv()
+        relay[p, -1].wait_recv()
+        for t in (1, -1):
+            second[p, 2, t] = send_to(block(p, 2, 0), block(p, 2, 0), near(d2, t))
+        share(p, 2, 0)
+    for o in (0, -1, 1, 2):
+        for s, start in ((1, 0), (-1, quarter)):
+            for p in (0, 1):
+                d1, d2, _ = plans[p]
+                second[p, o, s].wait_recv()
+                piece = block(p, o, -s, start, quarter)
+                relay2[p, o, s] = send_to(piece, piece, near(d2, s))
+                share(p, o, -s)
+
+    for move in lines:
+        move.wait_recv()
+    rows_in = jnp.concatenate(
+        [unit[:, 0:D]] + [line[d, :, 0:D] for d in range(tps - 1)], axis=0
+    )
+    hidden = silu(jnp.dot(rows_in, sgu[0], preferred_element_type=F32)) * jnp.dot(
+        rows_in, sgu[1], preferred_element_type=F32
+    )
+    hidden = hidden.astype(BF)
+    cut = D // tps
+    for b in range(tps):
+        piece = jnp.dot(
+            hidden, sdn[:, b * cut : (b + 1) * cut], preferred_element_type=F32
+        )
+        for j in range(tps):
+            some = piece[j * rows : (j + 1) * rows]
+            if j == 0:
+                some = some + resid[:, b * cut : (b + 1) * cut]
+            sh_out[b, wrap(mt - j, tps)] = some.astype(BF)
+    spread = []
+
+    def to_line(src, dst, k, i):
+        peer = lax.rem(mt + k, tps)
+        move = pltpu.make_async_remote_copy(
+            src_ref=src.at[peer], dst_ref=dst.at[k - 1], send_sem=tp_send.at[i],
+            recv_sem=tp_recv.at[i], device_id={"tp": peer}, device_id_type=MESH,
+        )
+        move.start()
+        return move
+
+    for k in (2, 1, 3):
+        spread.append(to_line(sh_out, sh_in, k, tps - 1 + k - 1))
+    for o in (0, -1, 1, 2):
+        for p in (0, 1):
+            relay2[p, o, 1].wait_recv()
+            relay2[p, o, -1].wait_recv()
+            share(p, o, 2)
+    for copy in loads:
+        copy.wait()
+    for move in far:
+        move.wait()
+    for move in list(first.values()) + list(second.values()):
+        move.wait_send()
+    for move in list(relay.values()) + list(relay2.values()):
+        move.wait_send()
+    for move in later:
+        if not any(move is m for m in lines):
+            move.wait()
+    for move in lines:
+        move.wait_send()
+
+    width = tps * wide
+    tile_rows = NY * rows
+
+    def expert_tile(xi, ci):
+        block_in = plane[:, xi, ci].reshape(tile_rows, D + LANES)
+        data = block_in[:, 0:D]
+        names = block_in[:, D:].astype(F32)
+        lane = lax.broadcasted_iota(jnp.int32, names.shape, 1)
+        total = None
+        for e in range(experts):
+            wt = jnp.sum(jnp.where(lane == me * experts + e, names, 0.0), axis=1, keepdims=True)
+            both = jnp.dot(data, gu[e], preferred_element_type=F32)
+            act = (silu(both[:, :width]) * both[:, width:] * wt).astype(BF)
+            part = jnp.dot(act, dn[e], preferred_element_type=F32)
+            total = part if total is None else total + part
+        return total.reshape(NY, rows, D)
+
+    def core_move(i):
+        xi = wrap(x + 2 - i, NX)
+        return pltpu.make_async_remote_copy(
+            src_ref=away.at[:, xi], dst_ref=partner.at[:, xi], send_sem=core_send.at[i],
+            recv_sem=core_recv.at[i], device_id={"seq": near("c", 1)}, device_id_type=MESH,
+        )
+
+    def partner_tile(i, carry):
+        xi = wrap(x + 2 - i, NX)
+        away[:, xi] = expert_tile(xi, 1 - c).astype(BF)
+        core_move(i).start()
+        return carry
+
+    lax.fori_loop(0, NX, partner_tile, 0)
+
+    def own_tile(i, carry):
+        xi = wrap(x + 2 - i, NX)
+        total = expert_tile(xi, c)
+        core_move(i).wait()
+        sums[:, xi] = (total + partner[:, xi].astype(F32)).astype(BF)
+        return carry
+
+    lax.fori_loop(0, NX, own_tile, 0)
+
+    plans = (("x", "y", 0), ("y", "x", half))
+
+    def row_line(d, o, r0, size):
+        if d == "x":
+            return sums.at[:, wrap(x + o, NX), pl.ds(r0, size)]
+        return sums.at[wrap(y + o, NY), :, pl.ds(r0, size)]
+
+    def cell(d, o, r0, size):
+        if d == "x":
+            return sums.at[y, wrap(x + o, NX), pl.ds(r0, size)]
+        return sums.at[wrap(y + o, NY), x, pl.ds(r0, size)]
+
+    def add(ref, *others):
+        value = ref[...].astype(F32)
+        for other in others:
+            value = value + other[...].astype(F32)
+        ref[...] = value.astype(BF)
+
+    done = []
+    final = [None, None]
+
+    def reduce_stage(pick, which, b_buf, a_buf, last):
+        bs_, as_ = {}, {}
+        for p in (0, 1):
+            d, r0 = plans[p][which], plans[p][2]
+            bs_[p, 0] = send_to(pick(d, 2, r0, quarter), b_buf.at[p, 0], near(d, 1))
+            bs_[p, 1] = send_to(pick(d, 2, r0 + quarter, quarter), b_buf.at[p, 1], near(d, -1))
+        for p in (0, 1):
+            d, r0 = plans[p][which], plans[p][2]
+            bs_[p, 0].wait_recv()
+            add(pick(d, 1, r0, quarter), b_buf.at[p, 0])
+            as_[p, 0] = send_to(pick(d, 1, r0, half), a_buf.at[p, 0], near(d, 1))
+            bs_[p, 1].wait_recv()
+            add(pick(d, -1, r0 + quarter, quarter), b_buf.at[p, 1])
+            as_[p, 1] = send_to(pick(d, -1, r0, half), a_buf.at[p, 1], near(d, -1))
+        for p in (0, 1):
+            d, r0 = plans[p][which], plans[p][2]
+            as_[p, 0].wait_recv()
+            as_[p, 1].wait_recv()
+            if last:
+                final[p] = (
+                    pick(d, 0, r0, half)[...].astype(F32)
+                    + a_buf[p, 0].astype(F32)
+                    + a_buf[p, 1].astype(F32)
                 )
-        return out
-
-    @pl.when(pl.program_id(0) == 0)
-    def _():
-        for copy in copies():
-            copy.start()
-        for copy in copies():
-            copy.wait()
-
-    x = x_ref[...]
-    total = None
-    hidden = parts * wide
-    for e in range(experts):
-        both = jnp.dot(x, gu[e], preferred_element_type=F32)
-        act = (silu(both[:, :hidden]) * both[:, hidden:] * w_ref[:, e : e + 1]).astype(BF)
-        out = jnp.dot(act, dn[e], preferred_element_type=F32)
-        total = out if total is None else total + out
-    o_ref[...] = total.astype(BF)
-
-
-def experts_dense(x, wts, gate_up, down):
-    rows = x.shape[0]
-    parts = len(gate_up)
-    experts, _, _, wide = gate_up[0].shape
-    tile = 256
-    hidden = parts * wide
+            else:
+                add(pick(d, 0, r0, half), a_buf.at[p, 0], a_buf.at[p, 1])
+        done.extend(bs_.values())
+        done.extend(as_.values())
+
+    reduce_stage(row_line, 0, b_in, a_in, False)
+    reduce_stage(cell, 1, b2_in, a2_in, True)
+    routed = jnp.concatenate(final, axis=0)
+    for b in range(tps):
+        fin_out[b] = routed[:, b * cut : (b + 1) * cut].astype(BF)
+    last = [to_line(fin_out, fin_in, k, 2 * (tps - 1) + k - 1) for k in (2, 1, 3)]
+    for move in spread:
+        move.wait()
+    total = sh_out[mt].astype(F32)
+    for k in range(tps - 1):
+        total = total + sh_in[k].astype(F32)
+    acc[...] = total
+    acc[mt] += fin_out[mt].astype(F32)
+    for move in last:
+        move.wait()
+    for k in range(1, tps):
+        acc[wrap(mt - k, tps)] += fin_in[k - 1].astype(F32)
+    for move in done:
+        move.wait_send()
+    out[...] = acc[...].reshape(tps * rows, cut).astype(BF)
+
+
+def experts(tps, unit, resid, gus, dns, shared_gate_up, shared_down):
+    rows = unit.shape[0]
+    count, _, _, wide = gus[0].shape
+    cut = D // tps
+    half, quarter = rows // 2, rows // 4
+    vm = pl.BlockSpec(memory_space=pltpu.VMEM)
+    hbm = pl.BlockSpec(memory_space=pl.ANY)
+    dma = pltpu.SemaphoreType.DMA
     return pl.pallas_call(
-        functools.partial(expert_kernel, parts),
-        out_shape=jax.ShapeDtypeStruct((rows, D), BF),
-        grid=(rows // tile,),
-        in_specs=[
-            pl.BlockSpec((tile, D), lambda i: (i, 0)),
-            pl.BlockSpec((tile, experts), lambda i: (i, 0)),
-        ]
-        + [pl.BlockSpec(memory_space=pl.ANY)] * (2 * parts),
-        out_specs=pl.BlockSpec((tile, D), lambda i: (i, 0)),
+        functools.partial(moe_kernel, tps),
+        out_shape=jax.ShapeDtypeStruct((tps * rows, cut), BF),
+        in_specs=[vm, vm] + [hbm] * 6 + [vm, vm],
+        out_specs=vm,
         scratch_shapes=[
-            pltpu.VMEM((experts, D, 2 * hidden), BF),
-            pltpu.VMEM((experts, hidden, D), BF),
-            pltpu.SemaphoreType.DMA((parts * experts * 3,)),
+            pltpu.VMEM((NY, NX, NC, rows, D + LANES), BF),
+            pltpu.VMEM((tps - 1, rows, D + LANES), BF),
+            pltpu.VMEM((count, D, 2 * tps * wide), BF),
+            pltpu.VMEM((count, tps * wide, D), BF),
+            pltpu.VMEM((NY, NX, rows, D), BF),
+            pltpu.VMEM((NY, NX, rows, D), BF),
+            pltpu.VMEM((NY, NX, rows, D), BF),
+            pltpu.VMEM((2, 2, NX, quarter, D), BF),
+            pltpu.VMEM((2, 2, NX, half, D), BF),
+            pltpu.VMEM((2, 2, quarter, D), BF),
+            pltpu.VMEM((2, 2, half, D), BF),
+            pltpu.VMEM((tps, tps, rows, cut), BF),
+            pltpu.VMEM((tps - 1, tps, rows, cut), BF),
+            pltpu.VMEM((tps, rows, cut), BF),
+            pltpu.VMEM((tps - 1, rows, cut), BF),
+            pltpu.VMEM((tps, rows, cut), F32),
+            dma((96,)),
+            dma((96,)),
+            dma((3 * (tps - 1),)),
+            dma((3 * (tps - 1),)),
+            dma((3 * count,)),
+            dma((3 * count,)),
+            dma((9 * count,)),
+            dma((NX,)),
+            dma((NX,)),
         ],
-        compiler_params=pltpu.CompilerParams(vmem_limit_bytes=40 << 20),
-        name="experts_dense",
-    )(x, wts, *gate_up, *down)
+        compiler_params=pltpu.CompilerParams(
+            collective_id=1, has_side_effects=True, vmem_limit_bytes=60 << 20
+        ),
+        name="experts",
+    )(unit, resid, *gus, *dns, shared_gate_up, shared_down)
 
 
 def body(
@@ -355,12 +648,10 @@
     expert_down, shared_gate_up, shared_down,
 ):
     rows = tokens.shape[0]
-    tp_index, seq_index = lax.axis_index("tp"), lax.axis_index("seq")
+    tp_index = lax.axis_index("tp")
     tp_count, seq_count = lax.axis_size("tp"), lax.axis_size("seq")
     heads = dt_proj.shape[1]
-    width = heads * HEAD
     part = rows // tp_count
-    experts_local = expert_down.shape[0]
 
     def shift(value, steps):
         pairs = [(t, (t + steps) % tp_count) for t in range(tp_count)]
@@ -369,8 +660,6 @@
     gu_left, dn_left = shift(expert_gate_up, 1), shift(expert_down, 1)
     gu_right, dn_right = shift(expert_gate_up, -1), shift(expert_down, -1)
     own_routes = lax.dynamic_slice_in_dim(routes, tp_index * part, part, 0)
-    plane_routes = lax.all_gather(own_routes, "seq", tiled=True)
-
     resid_in = tokens.astype(F32)
     normed_in = rms_apply(resid_in, mix_gain).astype(BF)
     zgate = jnp.dot(normed_in, zgate_proj, preferred_element_type=F32).astype(BF)
@@ -381,39 +670,16 @@
     rate = jnp.pad(decay_rate, (0, 128 - heads))[None, :]
     own_rows = lax.dynamic_slice_in_dim(tokens, tp_index * part, part, 0)
     ids = doc_ids.astype(F32)
-    resid, moe_in = mixer(
+    resid, unit = mixer(
         seq_count, tp_count, heads, x_pre, bc_pre, ids[:, None], ids[None, :], dt_raw, rate,
         conv_x.astype(F32), conv_bc.astype(F32), jnp.repeat(skip_gain, HEAD)[None, :], zgate,
         norm_gain.astype(F32)[None, :], out_proj, own_rows, moe_gain.astype(F32)[None, :],
-    )
-    moe_in, resid, gu_left, dn_right = lax.optimization_barrier(
-        (moe_in, resid, gu_left, dn_right)
-    )
-    gu_far, dn_far = shift(gu_left, 1), shift(dn_right, -1)
-
-    plane = lax.all_gather(moe_in, "seq", tiled=True)
-    line = lax.all_gather(moe_in, "tp", tiled=True)
-    logits = jnp.dot(plane, router, preferred_element_type=F32)
-    iota = jnp.arange(router.shape[1], dtype=jnp.int32)
-    named = jnp.any(plane_routes[:, :, None] == iota[None, None, :], axis=1)
-    sigmas = jnp.where(named, jax.nn.sigmoid(logits), 0.0)
-    wts = sigmas / jnp.sum(sigmas, axis=1, keepdims=True)
-    wts = lax.dynamic_slice_in_dim(wts, seq_index * experts_local, experts_local, 1)
-    routed = experts_dense(
-        plane, wts, (expert_gate_up, gu_left, gu_right, gu_far),
-        (expert_down, dn_left, dn_right, dn_far),
-    )
-    routed = lax.psum_scatter(routed, "seq", scatter_dimension=0, tiled=True)
-    shared_gate = jnp.dot(line, shared_gate_up[0], preferred_element_type=F32)
-    shared_up = jnp.dot(line, shared_gate_up[1], preferred_element_type=F32)
-    shared_act = (jax.nn.silu(shared_gate) * shared_up).astype(BF)
-    shared_part = jnp.dot(shared_act, shared_down, preferred_element_type=F32)
-    mine = lax.dynamic_slice_in_dim(shared_part, tp_index * part, part, 0)
-    whole = lax.dynamic_update_slice_in_dim(
-        shared_part, mine + resid + routed.astype(F32), tp_index * part, 0
-    )
-    added = lax.psum_scatter(whole, "tp", scatter_dimension=1, tiled=True)
-    return added.astype(BF)
+        router, own_routes,
+    )
+    return experts(
+        tp_count, unit, resid, (expert_gate_up, gu_left, gu_right),
+        (expert_down, dn_left, dn_right), shared_gate_up, shared_down,
+    )
 
 
 def solution(mesh):

time: 271 us -> 168 us (0.62)
  waiting for transfers between devices: 107 us -> 0.01 us
  Pallas kernels: 71.6 us -> 142 us
  blocking collectives: 38 us -> 0 us
  between operations: 13.3 us -> 0.17 us
  matrix products: 16.6 us -> 5.87 us
  other arithmetic: 7.93 us -> 3.25 us
  local copies, waits for them, and re-layouts: 6.1 us -> 9.07 us
    reduce_scatter x2 -> x0, waiting for transfers between devices: 88.2 us -> none  [the longest x1 62.3 us: body(): routed = lax.psum_scatter(routed, 'seq', scatter_dimension=0, tiled=True)]
    pallas_call x1, Pallas kernels: 28 us -> 98.1 us  [experts(): pl.pallas_call(functools.partial(moe_kernel, tps), out_shape=jax.ShapeDty...]
    all_gather x2 -> x0, blocking collectives: 38 us -> none  [the longest x1 23.9 us: body(): plane_routes = lax.all_gather(own_routes, 'seq', tiled=True)]
    all_gather x1 -> x0, waiting for transfers between devices: 16.5 us -> none  [body(): plane = lax.all_gather(moe_in, 'seq', tiled=True)]
    dot_general x3 -> x0, matrix products: 10.7 us -> none  [the longest x1 4.66 us: body(): logits = jnp.dot(plane, router, preferred_element_type=F32)]
    ppermute x6 -> x4, waiting for transfers between devices: 2.74 us -> 0.01 us  [shift(): return lax.ppermute(value, 'tp', pairs)]
    ppermute x6 -> x4, starting transfers between devices: 9.95 us -> 7.47 us  [shift(): return lax.ppermute(value, 'tp', pairs)]
  transfers between devices with their start and end apart: 9 -> 4, of which waited for: 4 -> 0; matrix products, arithmetic and copies ran while one was open for 10% -> 10% of each run, Pallas kernels for 16% -> 26%
where the time goes in v3:
time: 168 us
  Pallas kernels  142 us (85%)
  local copies, waits for them, and re-layouts  9.07 us (5%)
  starting transfers between devices  7.47 us (4%)
  matrix products  5.87 us (3%)
  other arithmetic  3.25 us (2%)
    pallas_call x1, Pallas kernels, experts(): pl.pallas_call(functools.partial(moe_kernel, tps), out_shape=jax.ShapeDty...  98.1 us
    pallas_call x1, Pallas kernels, mixer(): pl.pallas_call(functools.partial(mixer_kernel, heads, seqs, tps), out_sha...  43.8 us
    ppermute x4, starting transfers between devices, shift(): return lax.ppermute(value, 'tp', pairs)  7.47 us
    unnamed x31, local copies, waits for them, and re-layouts  3.4 us
  transfers between devices with their start and end apart: 4, of which 0 were waited for; matrix products, arithmetic and copies ran while one was open for 10% of the time, Pallas kernels for 26%

profile of v3, /device:TPU:0, one launch (start us, length us, event | category | flops | bytes accessed | tf_op | source)
XLA Modules:
  0.0 167.7 jit_solution(13647416231117838384)
XLA Ops:
  0.0 2.0 %collective-permute-start.2 = (bf16[2,128,1536]{2,1,0:T(8,128)(2,1)}, bf16[2,128,1536]{2,1,0:T(8,128)(2,1)}, u32[]{:S(2)}, u32[]{:S(2)}) collective-permute-start(bf16[2,128,1536]{2,1,0:T(8,128)(2,1)} %dn_own.1), channel_id=1, source_target_pairs={{0,1},{1,2},{2,3},{3,0},{4,5},{5,6},{6,7},{7,4},{8,9},{9,10},{10,1... | collective-permute-start | bytes 2359304 | tf_op jit(solution)/shard_map/ppermute | solution.py:658
  2.0 2.2 %collective-permute-start.3 = (bf16[2,128,1536]{2,1,0:T(8,128)(2,1)}, bf16[2,128,1536]{2,1,0:T(8,128)(2,1)}, u32[]{:S(2)}, u32[]{:S(2)}) collective-permute-start(bf16[2,128,1536]{2,1,0:T(8,128)(2,1)} %dn_own.1), channel_id=1, source_target_pairs={{0,3},{1,0},{2,1},{3,2},{4,7},{5,4},{6,5},{7,6},{8,11},{9,8},{10,9... | collective-permute-start | bytes 2359304 | tf_op jit(solution)/shard_map/ppermute | solution.py:658
  4.2 3.2 %collective-permute-start.1 = (bf16[2,2,1536,128]{3,2,1,0:T(8,128)(2,1)}, bf16[2,2,1536,128]{3,2,1,0:T(8,128)(2,1)}, u32[]{:S(2)}, u32[]{:S(2)}) collective-permute-start(bf16[2,2,1536,128]{3,2,1,0:T(8,128)(2,1)} %gu_own.1), channel_id=1, source_target_pairs={{0,3},{1,0},{2,1},{3,2},{4,7},{5,4},{6,5},{7,6},{8,11},{9,8},{10,9... | collective-permute-start | bytes 4718600 | tf_op jit(solution)/shard_map/ppermute | solution.py:658
  7.5 1.4 fusion
  8.8 0.7 convert_element_type.34
  9.5 1.7 %constant_dynamic-slice_fusion.1.tok_ref = bf16[64,1536]{1,0:T(8,128)(2,1)} fusion(bf16[256,1536]{1,0:T(8,128)(2,1)} %param.21, s32[]{:T(128)S(6)} %select_n.4), kind=kLoop, calls=%fused_computation.11 | loop fusion | bytes 393220 | tf_op jit(solution)/shard_map/dynamic_slice | solution.py:671
  11.2 1.6 convolution_add_fusion
  12.8 0.0 copy-start.7
  12.9 0.0 copy-start.9
  12.9 0.0 copy-start.8
  12.9 0.0 copy-start.10
  12.9 0.0 copy-start.4
  12.9 0.0 copy-start.13
  13.0 1.1 convolution_convert_fusion.2.bc_ref
  14.0 0.1 constant_dynamic-slice_fusion
  14.1 0.6 reshape.10.gain_ref
  14.7 0.6 convert_element_type.40.cb_ref
  15.3 0.6 reshape.11.moe_gain_ref
  15.9 0.1 broadcast_in_dim.28
  16.0 0.7 broadcast_in_dim_reshape.3.skip_ref
  16.7 0.6 convert_element_type.39.cx_ref
  17.3 0.7 copy.35.routes_ref
  18.0 0.8 copy.32.idc_ref
  18.8 0.9 copy.33.router_ref
  19.7 0.6 pad.8.dt_ref
  20.4 0.5 pad_bitcast_fusion.rate_ref
  20.9 1.6 convolution_convert_fusion.z_ref
  22.5 0.1 copy-done.11
  22.6 1.6 convolution_convert_fusion.1.x_ref
  24.1 43.8 %mixer.1 = (f32[64,1536]{1,0:T(8,128)}, bf16[64,1664]{1,0:T(8,128)(2,1)}) custom-call(bf16[256,768]{1,0:T(8,128)(2,1)} %convolution_convert_fusion.1.x_ref, bf16[256,256]{1,0:T(8,128)(2,1)} %convolution_convert_fusion.2.bc_ref, f32[256,1]{1,0:T(8,128)} %copy.32.idc_ref, f32[1,256]{1,0:T(1,128)} %bitcast.9, f32[256,128]{1,0:T(8,128)} %pad.8.dt_ref, ...), custom_call_target="tpu_custom_call" | custom-call | tf_op jit(solution)/shard_map/mixer/pallas_call | solution.py:260
  68.0 98.1 %experts.1 = bf16[256,384]{1,0:T(8,128)(2,1)} custom-call(bf16[64,1664]{1,0:T(8,128)(2,1)} %get-tuple-element.7.unit, f32[64,1536]{1,0:T(8,128)} %get-tuple-element.8.resid, bf16[2,2,1536,128]{3,2,1,0:T(8,128)(2,1)} %gu_own.1, bf16[2,2,1536,128]{3,2,1,0:T(8,128)(2,1)} %collective-permute-done.gu_left, ...), custom_call_target="tpu_custom_call" | custom-call | tf_op jit(solution)/shard_map/experts/pallas_call | solution.py:606
  166.1 1.6 copy.37
  (28 shorter events, 0.1 us)
Async XLA Ops:
  0.0 20.9 %copy-start = (bf16[1536,768]{1,0:T(8,128)(2,1)S(1)}, bf16[1536,768]{1,0:T(8,128)(2,1)}, u32[]{:S(2)}) copy-start(bf16[1536,768]{1,0:T(8,128)(2,1)} %param.24) | copy-start | bytes 7077892
  0.0 12.8 %copy-start.1 = (bf16[256,1536]{1,0:T(8,128)(2,1)S(1)}, bf16[256,1536]{1,0:T(8,128)(2,1)}, u32[]{:S(2)}) copy-start(bf16[256,1536]{1,0:T(8,128)(2,1)} %param.21) | copy-start | bytes 2359300
  0.0 67.9 %collective-permute-start.2 = (bf16[2,128,1536]{2,1,0:T(8,128)(2,1)}, bf16[2,128,1536]{2,1,0:T(8,128)(2,1)}, u32[]{:S(2)}, u32[]{:S(2)}) collective-permute-start(bf16[2,128,1536]{2,1,0:T(8,128)(2,1)} %dn_own.1), channel_id=1, source_target_pairs={{0,1},{1,2},{2,3},{3,0},{4,5},{5,6},{6,7},{7,4},{8,9},{9,10},{10,1... | collective-permute-start | bytes 2359304 | tf_op jit(solution)/shard_map/ppermute | solution.py:658
  2.0 65.9 %collective-permute-start.3 = (bf16[2,128,1536]{2,1,0:T(8,128)(2,1)}, bf16[2,128,1536]{2,1,0:T(8,128)(2,1)}, u32[]{:S(2)}, u32[]{:S(2)}) collective-permute-start(bf16[2,128,1536]{2,1,0:T(8,128)(2,1)} %dn_own.1), channel_id=1, source_target_pairs={{0,3},{1,0},{2,1},{3,2},{4,7},{5,4},{6,5},{7,6},{8,11},{9,8},{10,9... | collective-permute-start | bytes 2359304 | tf_op jit(solution)/shard_map/ppermute | solution.py:658
  4.2 63.7 %collective-permute-start = (bf16[2,2,1536,128]{3,2,1,0:T(8,128)(2,1)}, bf16[2,2,1536,128]{3,2,1,0:T(8,128)(2,1)}, u32[]{:S(2)}, u32[]{:S(2)}) collective-permute-start(bf16[2,2,1536,128]{3,2,1,0:T(8,128)(2,1)} %gu_own.1), channel_id=1, source_target_pairs={{0,1},{1,2},{2,3},{3,0},{4,5},{5,6},{6,7},{7,4},{8,9},{9,10},{10,1... | collective-permute-start | bytes 4718600 | tf_op jit(solution)/shard_map/ppermute | solution.py:658
  4.2 63.7 %collective-permute-start.1 = (bf16[2,2,1536,128]{3,2,1,0:T(8,128)(2,1)}, bf16[2,2,1536,128]{3,2,1,0:T(8,128)(2,1)}, u32[]{:S(2)}, u32[]{:S(2)}) collective-permute-start(bf16[2,2,1536,128]{3,2,1,0:T(8,128)(2,1)} %gu_own.1), channel_id=1, source_target_pairs={{0,3},{1,0},{2,1},{3,2},{4,7},{5,4},{6,5},{7,6},{8,11},{9,8},{10,9... | collective-permute-start | bytes 4718600 | tf_op jit(solution)/shard_map/ppermute | solution.py:658
  9.5 3.3 %copy-start.12 = (bf16[1536,256]{1,0:T(8,128)(2,1)S(1)}, bf16[1536,256]{1,0:T(8,128)(2,1)}, u32[]{:S(2)}) copy-start(bf16[1536,256]{1,0:T(8,128)(2,1)} %param.26) | copy-start | bytes 2359300
  12.8 1.2 copy-start.7
  12.9 1.3 copy-start.9
  12.9 1.3 copy-start.8
  12.9 1.8 %copy-start.6 = (bf16[4,256]{1,0:T(4,128)(2,1)S(1)}, bf16[4,256]{1,0:T(4,128)(2,1)}, u32[]{:S(2)}) copy-start(bf16[4,256]{1,0:T(4,128)(2,1)} %param.29) | copy-start | bytes 6148
  12.9 2.4 %copy-start.5 = (bf16[1536]{0:T(1024)(128)(2,1)S(1)}, bf16[1536]{0:T(1024)(128)(2,1)}, u32[]{:S(2)}) copy-start(bf16[1536]{0:T(1024)(128)(2,1)} %param.35) | copy-start | bytes 9220
  12.9 3.0 %copy-start.10 = (f32[12]{0:T(128)S(1)}, f32[12]{0:T(128)}, u32[]{:S(2)}) copy-start(f32[12]{0:T(128)} %param.32) | copy-start | bytes 148
  12.9 3.7 %copy-start.4 = (bf16[4,768]{1,0:T(4,128)(2,1)S(1)}, bf16[4,768]{1,0:T(4,128)(2,1)}, u32[]{:S(2)}) copy-start(bf16[4,768]{1,0:T(4,128)(2,1)} %param.28) | copy-start | bytes 18436
  12.9 5.9 %copy-start.2 = (bf16[1536,64]{0,1:T(8,128)(2,1)S(1)}, bf16[1536,64]{0,1:T(8,128)(2,1)}, u32[]{:S(2)}) copy-start(bf16[1536,64]{0,1:T(8,128)(2,1)} %param.36) | copy-start | bytes 589828
  12.9 7.4 %copy-start.13 = (f32[12]{0:T(128)S(1)}, f32[12]{0:T(128)}, u32[]{:S(2)}) copy-start(f32[12]{0:T(128)} %param.31) | copy-start | bytes 148
  14.1 8.4 %copy-start.3 = (f32[256]{0:T(256)}, f32[256]{0:T(256)S(1)}, u32[]{:S(2)}) copy-start(f32[256]{0:T(256)S(1)} %convert_element_type.38) | copy-start | bytes 3076
  20.9 1.7 copy-start.11
